TPU v7x, 32 devices: a whole 2x2x4 slice. The times are simulated.
32 devices in a mesh: sec: 4 (over y, core), ctx: 2 (over x), tp: 4 (over z).
Axes of the slice: x: 2, y: 2, z: 4, core: 2. Of those that a mesh axis runs over, the one named last changes fastest.
Arguments:
- self_query: bfloat16 [1024, 2048], P('ctx', ('sec', 'tp')), may hold values from -6 to 6
- self_key: bfloat16 [1024, 2048], P('ctx', ('sec', 'tp')), may hold values from -6 to 6
- self_value: bfloat16 [1024, 2048], P('ctx', ('sec', 'tp')), may hold values from -6 to 6
- self_gain: float32 [2048], P(('sec', 'tp')), may hold values from 0.5 to 1.5
- self_grad: bfloat16 [1024, 2048], P('ctx', ('sec', 'tp')), may hold values from -6 to 6
- cross_query: bfloat16 [1024, 2048], P('ctx', ('sec', 'tp')), may hold values from -6 to 6
- memory_key: bfloat16 [256, 2048], P(('sec', 'ctx')), may hold values from -6 to 6
- memory_value: bfloat16 [256, 2048], P(('sec', 'ctx')), may hold values from -6 to 6
- cross_gain: float32 [2048], P(('sec', 'tp')), may hold values from 0.5 to 1.5
- cross_grad: bfloat16 [1024, 2048], P('ctx', ('sec', 'tp')), may hold values from -6 to 6
- block_start: int32 [8], replicated, may hold values from 0 to 7, each once
Outputs:
- self_out: bfloat16 [1024, 2048], P('ctx', ('sec', 'tp'))
- cross_out: bfloat16 [1024, 2048], P('ctx', ('sec', 'tp'))
- query_grad: bfloat16 [1024, 2048], P('ctx', ('sec', 'tp'))
- key_grad: bfloat16 [1024, 2048], P('ctx', ('sec', 'tp'))
- value_grad: bfloat16 [1024, 2048], P('ctx', ('sec', 'tp'))
- cross_query_grad: bfloat16 [1024, 2048], P('ctx', ('sec', 'tp'))
- memory_key_grad: bfloat16 [256, 2048], P(('sec', 'ctx'))
- memory_value_grad: bfloat16 [256, 2048], P(('sec', 'ctx'))
Inputs may be any that keep to these rules, and one draw needn't show every extreme that they name: `block_start`: every number appears once.
All inputs are finite; a program needn't handle non-finite values.
Results may differ from a plain program's by a relative error of at most 0.015.
Values may be sent and summed in bfloat16 or wider, within the bound.
No kernel may reach another device: no remote copies, remote signals or barrier semaphores. Data moves between devices by JAX's collectives and lax.ppermute only.
A program may use at most 64 MiB of HBM per device.

v0:
```python
import math

import jax
import jax.numpy as jnp
from jax import lax
from jax.experimental import pallas as pl
from jax.experimental.pallas import tpu as pltpu
from jax.sharding import PartitionSpec as P


EPS = 1e-06
F32 = jnp.float32
BF16 = jnp.bfloat16
VMEM = pl.BlockSpec(memory_space=pltpu.VMEM)
ROOM = 4 << 20
LIMIT = 60 << 20
SMEM = pl.BlockSpec(memory_space=pltpu.SMEM)
HBM = pl.BlockSpec(memory_space=pltpu.HBM)


def call(body, inputs, outputs, flops=0, scratch=(), smem=0, after=(), loads=False):
    waits = len(after)
    if waits:
        inner, count = body, len(inputs)

        def body(*refs):
            inner(*refs[:count], *refs[count + waits :])

    moved = sum(math.prod(shape) * jnp.dtype(kind).itemsize for shape, kind in outputs)
    moved += sum(entry.size * entry.dtype.itemsize for entry in inputs)
    held = sum(
        math.prod(entry.shape) * jnp.dtype(entry.dtype).itemsize
        for entry in scratch
        if jnp.issubdtype(entry.dtype, jnp.number)
    )
    if loads:
        inputs = [pltpu.with_memory_space_constraint(entry, pltpu.HBM) for entry in inputs]
        shapes = [pltpu.VMEM(shape, kind) for shape, kind in outputs]
    else:
        shapes = [jax.ShapeDtypeStruct(shape, kind) for shape, kind in outputs]
    space = HBM if loads else VMEM
    return list(
        pl.pallas_call(
            body,
            out_shape=shapes,
            in_specs=[SMEM] * smem + [space] * (len(inputs) - smem) + [VMEM] * waits,
            out_specs=[VMEM] * len(outputs),
            scratch_shapes=list(scratch),
            cost_estimate=pl.CostEstimate(flops=flops, bytes_accessed=moved, transcendentals=0),
            compiler_params=pltpu.CompilerParams(
                vmem_limit_bytes=min(2 * (moved + held) + ROOM, LIMIT)
            ),
        )(*inputs, *after)
    )


def dot_nt(left, right):
    return lax.dot_general(left, right, (((1,), (1,)), ((), ())), preferred_element_type=F32)


def dot_nn(left, right):
    return lax.dot_general(left, right, (((1,), (0,)), ((), ())), preferred_element_type=F32)


def dot_tn(left, right):
    return lax.dot_general(left, right, (((0,), (0,)), ((), ())), preferred_element_type=F32)


def row_positions(bases, quarter):
    lanes = lax.broadcasted_iota(jnp.int32, (1, quarter), 1)
    parts = [bases[part : part + 1, part * quarter : (part + 1) * quarter] + lanes for part in range(4)]
    return jnp.concatenate(parts, axis=1)


def fold_block(key, value, queries, running, store, masks, held, scaling):
    rows, step = key.shape[0], 128
    step = min(step, rows)
    top, total, weighted = running
    block_top = top
    for at in range(0, rows, step):
        scores = dot_nt(key[at : at + step, :], queries) * scaling
        if masks is not None:
            key_first, query_positions = masks
            down = lax.broadcasted_iota(jnp.int32, (step, 1), 0)
            scores = jnp.where(down > query_positions - key_first(at), -jnp.inf, scores)
        held[at : at + step, :] = scores
        block_max = jnp.max(scores, axis=0, keepdims=True)
        block_top = block_max if block_top is None else jnp.maximum(block_top, block_max)
    block_total = None
    for at in range(0, rows, step):
        raised = jnp.exp(held[at : at + step, :] - block_top)
        part = jnp.sum(raised, axis=0, keepdims=True)
        block_total = part if block_total is None else block_total + part
        store[at : at + step, :] = raised.astype(BF16)
    product = dot_tn(value[...], store[...])
    if top is None:
        return block_top, block_total, product
    shrink = jnp.exp(top - block_top)
    return block_top, total * shrink + block_total, weighted * shrink + product


def solution(mesh):
    sections, contexts, tensors = mesh.shape["sec"], mesh.shape["ctx"], mesh.shape["tp"]
    peers = sections * tensors

    def shifted(value, axis, count, by):
        return lax.ppermute(value, axis, [(at, (at + by) % count) for at in range(count)])

    def paired(at, by, count):
        return jnp.bitwise_xor(at, by) if count & (count - 1) == 0 else lax.rem(at + by, count)

    def unpaired(at, by, count):
        return jnp.bitwise_xor(at, by) if count & (count - 1) == 0 else lax.rem(at - by + count, count)

    def swapped(value, axis, count, by, back=False):
        if count & (count - 1) == 0:
            return lax.ppermute(value, axis, [(at, at ^ by) for at in range(count)])
        return shifted(value, axis, count, -by if back else by)

    def over_sections(value, by, back=False):
        return swapped(value, "sec", sections, by, back)

    def over_tensors(value, by):
        return swapped(value, "tp", tensors, by)

    def per_device(
        self_query,
        self_key,
        self_value,
        self_gain,
        self_grad,
        cross_query,
        memory_key,
        memory_value,
        cross_gain,
        cross_grad,
        block_start,
    ):
        frames, columns = self_query.shape
        rows = memory_key.shape[0]
        quarter = frames // 4
        full_width = columns * peers
        group = sections * rows
        others = contexts - 1
        scaling = 1.0 / math.sqrt(columns)
        wide = (frames, columns)
        tall = (columns, frames)
        line = (1, frames)
        unit = 2 * frames * columns

        def copy_all(moves, semaphores, meanwhile=None):
            copies = [
                pltpu.make_async_copy(source, target, semaphores.at[at])
                for at, (source, target) in enumerate(moves)
            ]
            for copy in copies:
                copy.start()
            if meanwhile:
                meanwhile()
            for copy in copies:
                copy.wait()

        def load_memory(key_ref, value_ref, *refs):
            outs, semaphores = refs[:-1], refs[-1]
            section, tensor = lax.axis_index("sec"), lax.axis_index("tp")
            moves = []
            for by, out in enumerate(outs):
                head = paired(section, by, sections) * tensors + tensor
                at = pl.ds(pl.multiple_of(head * columns, columns), columns)
                moves += [(key_ref.at[:, at], out.at[0]), (value_ref.at[:, at], out.at[1])]
            copy_all(moves, semaphores)

        pieces = call(
            load_memory,
            [memory_key, memory_value],
            [((2, rows, columns), BF16)] * sections,
            scratch=[pltpu.SemaphoreType.DMA((2 * sections,))],
            loads=True,
        )

        plain = [
            self_query,
            self_key,
            self_value,
            self_grad,
            cross_query,
            cross_grad,
            self_gain.reshape(1, columns),
            cross_gain.reshape(1, columns),
        ]

        def load_rows(starts, *refs):
            count = len(plain)
            bases, semaphores = refs[-2:]

            def positions():
                context = lax.axis_index("ctx")
                for by in range(contexts):
                    source = lax.rem(context - by + contexts, contexts)
                    for part in range(4):
                        at = by * 4 + part
                        first = starts[source * 4 + part] * quarter
                        bases[at : at + 1, :] = jnp.full((1, frames), first, jnp.int32)

            copy_all(list(zip(refs[:count], refs[count : 2 * count])), semaphores, positions)

        other_keys = [shifted(self_key, "ctx", contexts, by) for by in range(1, contexts)]
        other_values = [shifted(self_value, "ctx", contexts, by) for by in range(1, contexts)]

        results = call(
            load_rows,
            [block_start] + plain,
            [(entry.shape, entry.dtype) for entry in plain] + [((4 * contexts, frames), jnp.int32)],
            scratch=[pltpu.SemaphoreType.DMA((len(plain),))],
            smem=1,
            loads=True,
        )
        self_query, self_key, self_value, self_grad, cross_query, cross_grad, self_gain, cross_gain, bases = results

        arrived = [pieces[0]] + [over_sections(pieces[by], by) for by in range(1, sections)]

        def gather(*refs):
            out = refs[-1]
            for at, ref in enumerate(refs[:-1]):
                out[:, at * rows : (at + 1) * rows, :] = ref[...]

        (own_memory,) = call(gather, arrived, [((2, group, columns), BF16)])
        memories = [own_memory] + [
            shifted(own_memory, "ctx", contexts, by) for by in range(1, contexts)
        ]

        def first_block(
            base,
            query,
            key,
            value,
            gain,
            grad,
            cross_gain_ref,
            cross_grad_ref,
            store,
            top,
            total,
            weighted,
            lifted,
            cross_lifted_ref,
            held,
        ):
            masks = (
                lambda at: base[at // quarter : at // quarter + 1, :] + at % quarter,
                row_positions(base, quarter),
            )
            top[...], total[...], weighted[...] = fold_block(
                key, value, query[...], (None, None, None), store, masks, held, scaling
            )
            lifted[...] = (gain[...] * grad[...].astype(F32)).T
            cross_lifted_ref[...] = (cross_gain_ref[...] * cross_grad_ref[...].astype(F32)).T

        first_store, first_top, first_total, first_weighted, self_lifted, cross_lifted = call(
            first_block,
            [
                bases,
                self_query,
                self_key,
                self_value,
                self_gain,
                self_grad,
                cross_gain,
                cross_grad,
            ],
            [((frames, frames), BF16), (line, F32), (line, F32), (tall, F32), (tall, F32), (tall, F32)],
            flops=2 * frames * unit,
            scratch=[pltpu.VMEM((frames, frames), F32)],
        )

        def statistics(attended, lifted):
            return (
                jnp.sum(attended * attended, axis=0, keepdims=True),
                jnp.sum(lifted * attended, axis=0, keepdims=True),
            )

        def other_blocks(base, query, top, total, weighted, lifted, *refs):
            keys, values = refs[:others], refs[others : 2 * others]
            stores = refs[2 * others : 3 * others]
            first_weight, weight, attended_ref, stats, held = refs[3 * others :]
            positions = row_positions(base, quarter)
            running = (top[...], total[...], weighted[...])
            tops = [top[...]]
            for by in range(others):
                first = 4 * (by + 1)
                masks = (
                    lambda at, first=first: base[first + at // quarter : first + at // quarter + 1, :]
                    + at % quarter,
                    positions,
                )
                running = fold_block(
                    keys[by], values[by], query[...], running, stores[by], masks, held, scaling
                )
                tops.append(running[0])
            last = 1.0 / running[1]
            first_weight[...] = jnp.exp(tops[0] - running[0]) * last
            for by in range(others):
                weight[by : by + 1, :] = jnp.exp(tops[by + 1] - running[0]) * last
            attended = running[2] * last
            attended_ref[...] = attended
            stats[0:1, :], stats[1:2, :] = statistics(attended, lifted[...])

        results = call(
            other_blocks,
            [bases, self_query, first_top, first_total, first_weighted, self_lifted]
            + other_keys
            + other_values,
            [((frames, frames), BF16)] * others
            + [(line, F32), ((others, frames), F32), (tall, F32), ((2, frames), F32)],
            flops=2 * frames * unit * others,
            scratch=[pltpu.VMEM((frames, frames), F32)],
        )
        other_stores = results[:others]
        first_weight, other_weight, self_attended, self_stats = results[others:]

        half = frames // 2

        def cross_forward(query, lifted, self_stats_ref, *refs):
            blocks, stores = refs[:contexts], refs[contexts : 2 * contexts]
            weight, attended_ref, stats, packed, held = refs[2 * contexts :]
            running = (None, None, None)
            tops = []
            for at in range(contexts):
                running = fold_block(
                    blocks[at].at[0], blocks[at].at[1], query[...], running, stores[at], None, held, scaling
                )
                tops.append(running[0])
            last = 1.0 / running[1]
            for at in range(contexts):
                weight[at : at + 1, :] = jnp.exp(tops[at] - running[0]) * last
            attended = running[2] * last
            attended_ref[...] = attended
            squares, slopes = statistics(attended, lifted[...])
            stats[0:1, :], stats[1:2, :] = squares, slopes
            lines = [self_stats_ref[0:1, :], self_stats_ref[1:2, :], squares, slopes]
            halves = [entry[:, at : at + half] for entry in lines for at in (0, half)]
            tile = jnp.concatenate(halves, axis=0)
            packed[...] = tile

        results = call(
            cross_forward,
            [cross_query, cross_lifted, self_stats] + memories,
            [((group, frames), BF16)] * contexts
            + [
                ((contexts, frames), F32),
                (tall, F32),
                ((2, frames), F32),
                ((8, half), F32),
            ],
            flops=2 * group * contexts * unit,
            scratch=[pltpu.VMEM((group, frames), F32)],
        )
        cross_stores = results[:contexts]
        cross_weight, cross_attended, cross_stats, packed = results[contexts:]

        def add_all(*refs):
            total = refs[0][...]
            for ref in refs[1:-1]:
                total = total + ref[...]
            refs[-1][...] = total

        near = [packed] + [over_sections(packed, by) for by in range(1, sections)]
        (partial,) = call(add_all, near, [((8, half), F32)])
        received = [partial] + [over_tensors(partial, by) for by in range(1, tensors)]

        def norm_terms(received_ref, stats, attended, lifted, at):
            sums = received_ref[0][...]
            for entry in received_ref[1:]:
                sums = sums + entry[...]
            joined = [
                jnp.concatenate([sums[2 * pick : 2 * pick + 1], sums[2 * pick + 1 : 2 * pick + 2]], axis=1)
                for pick in (2 * at, 2 * at + 1)
            ]
            scale = lax.rsqrt(joined[0] / full_width + EPS)
            slope = joined[1] / full_width
            curve = scale * scale * slope
            grad = scale * (lifted[...] - attended[...] * curve)
            delta = scale * (stats[1:2, :] - curve * stats[0:1, :])
            return scale, delta, grad

        def block_grads(key_grad, value_grad, value, store, weight, delta, grad_tall, grad_wide, query, slopes):
            count, step = value.shape[0], 128
            step = min(step, count)
            for at in range(0, count, step):
                products = dot_nn(value[at : at + step, :], grad_tall)
                probs = store[at : at + step, :]
                slope = (probs.astype(F32) * ((products - delta) * weight)).astype(BF16)
                slopes[at : at + step, :] = slope
                key_grad(at, step, dot_nn(slope, query) * scaling)
                value_grad(at, step, dot_nn(probs, grad_wide))

        def cross_backward(*refs):
            received_ref, (stats, attended, lifted, weight, query) = refs[:tensors], refs[tensors : tensors + 5]
            refs = refs[tensors + 5 :]
            blocks, stores = refs[:contexts], refs[contexts : 2 * contexts]
            sums, slopes, scale_ref = refs[2 * contexts : 3 * contexts], refs[3 * contexts : 4 * contexts], refs[-1]
            scale, delta, grad = norm_terms(received_ref, stats, attended, lifted, 1)
            scale_ref[...] = scale
            grad_tall = grad.astype(BF16)
            for at in range(contexts):
                line_weight = weight[at : at + 1, :]
                grad_wide = (grad * line_weight).T.astype(BF16)

                def key_grad(first, count, value, out=sums[at]):
                    out[0, first : first + count, :] = value.astype(out.dtype)

                def value_grad(first, count, value, out=sums[at]):
                    out[1, first : first + count, :] = value.astype(out.dtype)

                block_grads(
                    key_grad,
                    value_grad,
                    blocks[at].at[1],
                    stores[at],
                    line_weight,
                    delta,
                    grad_tall,
                    grad_wide,
                    query[...],
                    slopes[at],
                )

        results = call(
            cross_backward,
            received
            + [cross_stats, cross_attended, cross_lifted, cross_weight, cross_query]
            + memories
            + list(cross_stores),
            [((2, group, columns), F32)]
            + [((2, group, columns), BF16)] * others
            + [((group, frames), BF16)] * contexts
            + [(line, F32)],
            flops=3 * group * contexts * unit,
        )
        memory_sums, cross_slopes, cross_scale = results[:contexts], results[contexts:-1], results[-1]

        returned = [shifted(memory_sums[by], "ctx", contexts, -by) for by in range(1, contexts)]

        def add_up(*refs):
            own, extra, outs = refs[0], refs[1 : 1 + others], refs[1 + others :]
            for at, out in enumerate(outs):
                part = slice(at * rows, (at + 1) * rows)
                total = own[:, part, :]
                for entry in extra:
                    total = total + entry[:, part, :].astype(F32)
                out[...] = total.astype(BF16)

        parts = call(add_up, [memory_sums[0]] + returned, [((2, rows, columns), BF16)] * sections)
        back = [parts[0]] + [over_sections(parts[by], by, back=True) for by in range(1, sections)]

        def by_section(*refs):
            out = refs[-1]
            section = lax.axis_index("sec")
            for by, ref in enumerate(refs[:-1]):
                out[paired(section, by, sections)] = ref[...]

        (mine,) = call(by_section, back, [((sections, 2, rows, columns), BF16)])
        lines = [mine] + [over_tensors(mine, by) for by in range(1, tensors)]

        def assemble(*refs):
            sources, key_out, value_out = refs[:tensors], refs[tensors], refs[tensors + 1]
            tensor = lax.axis_index("tp")
            for by, ref in enumerate(sources):
                source = unpaired(tensor, by, tensors)
                for section in range(sections):
                    head = section * tensors + source
                    at = pl.ds(pl.multiple_of(head * columns, columns), columns)
                    key_out[:, at] = ref[section, 0]
                    value_out[:, at] = ref[section, 1]

        memory_key_grad, memory_value_grad = call(
            assemble, lines, [(memory_key.shape, BF16), (memory_value.shape, BF16)]
        )

        def other_backward(*refs):
            received_ref, (stats, attended, lifted, weight, query) = refs[:tensors], refs[tensors : tensors + 5]
            refs = refs[tensors + 5 :]
            values, stores = refs[:others], refs[others : 2 * others]
            pairs_out, slopes = refs[2 * others : 3 * others], refs[3 * others : 4 * others]
            grad_ref, scale_ref, delta_ref = refs[4 * others :]
            scale, delta, grad = norm_terms(received_ref, stats, attended, lifted, 0)
            scale_ref[...], delta_ref[...], grad_ref[...] = scale, delta, grad
            grad_tall = grad.astype(BF16)
            for by in range(others):
                line_weight = weight[by : by + 1, :]
                grad_wide = (grad * line_weight).T.astype(BF16)

                def key_grad(first, count, value, out=pairs_out[by]):
                    out[0, first : first + count, :] = value.astype(BF16)

                def value_grad(first, count, value, out=pairs_out[by]):
                    out[1, first : first + count, :] = value.astype(BF16)

                block_grads(
                    key_grad,
                    value_grad,
                    values[by],
                    stores[by],
                    line_weight,
                    delta,
                    grad_tall,
                    grad_wide,
                    query[...],
                    slopes[by],
                )

        results = call(
            other_backward,
            received
            + [self_stats, self_attended, self_lifted, other_weight, self_query]
            + other_values
            + list(other_stores),
            [((2,) + wide, BF16)] * others
            + [((frames, frames), BF16)] * others
            + [(tall, F32), (line, F32), (line, F32)],
            flops=3 * frames * unit * others,
            after=[cross_scale],
        )
        away, other_slopes = results[:others], results[others : 2 * others]
        self_attended_grad, self_scale, self_delta = results[2 * others :]
        home = [shifted(away[by], "ctx", contexts, -(by + 1)) for by in range(others)]

        def own_backward(grad, scale, delta, weight, gain, attended, query, key, value, store, *refs):
            keys, slopes = refs[:others], refs[others : 2 * others]
            key_out, value_out, query_out, out, own_slopes = refs[2 * others :]
            grad_tall = grad[...].astype(BF16)
            line_weight = weight[...]
            grad_wide = (grad[...] * line_weight).T.astype(BF16)

            def key_grad(first, count, result):
                key_out[first : first + count, :] = result

            def value_grad(first, count, result):
                value_out[first : first + count, :] = result

            block_grads(
                key_grad,
                value_grad,
                value,
                store,
                line_weight,
                delta[...],
                grad_tall,
                grad_wide,
                query[...],
                own_slopes,
            )
            total = dot_tn(key[...], own_slopes[...])
            for by in range(others):
                total = total + dot_tn(keys[by][...], slopes[by][...])
            query_out[...] = (total * scaling).T.astype(BF16)
            out[...] = (gain[...] * (attended[...] * scale[...]).T).astype(BF16)

        own_key, own_value, query_grad, self_out = call(
            own_backward,
            [
                self_attended_grad,
                self_scale,
                self_delta,
                first_weight,
                self_gain,
                self_attended,
                self_query,
                self_key,
                self_value,
                first_store,
            ]
            + other_keys
            + list(other_slopes),
            [(wide, F32), (wide, F32), (wide, BF16), (wide, BF16)],
            flops=(4 + others) * frames * unit,
            scratch=[pltpu.VMEM((frames, frames), BF16)],
        )

        def cross_rest(scale, gain, attended, *refs):
            blocks, slopes = refs[:contexts], refs[contexts : 2 * contexts]
            query_out, out = refs[2 * contexts :]
            total = dot_tn(blocks[0][0], slopes[0][...])
            for at in range(1, contexts):
                total = total + dot_tn(blocks[at][0], slopes[at][...])
            query_out[...] = (total * scaling).T.astype(BF16)
            out[...] = (gain[...] * (attended[...] * scale[...]).T).astype(BF16)

        cross_query_grad, cross_out = call(
            cross_rest,
            [cross_scale, cross_gain, cross_attended] + memories + list(cross_slopes),
            [(wide, BF16), (wide, BF16)],
            flops=group * contexts * unit,
        )

        def add_home(own_key_ref, own_value_ref, *refs):
            pairs, key_out, value_out = refs[:others], refs[others], refs[others + 1]
            for at, (own, out) in enumerate(((own_key_ref, key_out), (own_value_ref, value_out))):
                total = own[...]
                for pair in pairs:
                    total = total + pair[at].astype(F32)
                out[...] = total.astype(BF16)

        key_grad, value_grad = call(add_home, [own_key, own_value] + home, [(wide, BF16), (wide, BF16)])
        return (
            self_out,
            cross_out,
            query_grad,
            key_grad,
            value_grad,
            cross_query_grad,
            memory_key_grad,
            memory_value_grad,
        )

    rowed = P("ctx", ("sec", "tp"))
    stored = P(("sec", "ctx"), None)
    gains = P(("sec", "tp"))
    return jax.shard_map(
        per_device,
        mesh=mesh,
        in_specs=(rowed, rowed, rowed, gains, rowed, rowed, stored, stored, gains, rowed, P()),
        out_specs=(rowed, rowed, rowed, rowed, rowed, rowed, stored, stored),
        check_vma=False,
    )
```

profile of v0, /device:TPU:0, one launch (start us, length us, event | category | flops | bytes accessed | tf_op | source)
XLA Modules:
  0.0 52.3 jit_solution(1654725364734015497)
XLA Ops:
  0.6 3.0 %collective-permute-start = (bf16[512,128]{1,0:T(8,128)(2,1)}, bf16[512,128]{1,0:T(8,128)(2,1)S(1)}, u32[]{:S(2)}, u32[]{:S(2)}) collective-permute-start(bf16[512,128]{1,0:T(8,128)(2,1)} %refs_1_.1), channel_id=1, source_target_pairs={{0,4},{4,0},{1,5},{5,1},{2,6},{6,2},{3,7},{7,3},{8,12},{12,8},{9,1... | collective-permute-start | bytes 393224 | tf_op jit(solution)/shard_map/ppermute | solution.py:107
  3.7 0.9 %shard_map.173 = (bf16[2,32,128]{2,1,0:T(8,128)(2,1)S(1)}, bf16[2,32,128]{2,1,0:T(8,128)(2,1)S(1)}, bf16[2,32,128]{2,1,0:T(8,128)(2,1)S(1)}, bf16[2,32,128]{2,1,0:T(8,128)(2,1)S(1)}) custom-call(bf16[32,2048]{1,0:T(8,128)(2,1)} %key_ref.1, bf16[32,2048]{1,0:T(8,128)(2,1)} %value_ref.1), custom_call_target="tpu_custom_call" | custom-call | bytes 327680 | tf_op jit(solution)/shard_map/pallas_call | solution.py:43
  4.7 2.0 %collective-permute-start.3 = (bf16[2,32,128]{2,1,0:T(8,128)(2,1)S(1)}, bf16[2,32,128]{2,1,0:T(8,128)(2,1)S(1)}, u32[]{:S(2)}, u32[]{:S(2)}) collective-permute-start(bf16[2,32,128]{2,1,0:T(8,128)(2,1)S(1)} %get-tuple-element.79), channel_id=1, source_target_pairs={{0,16},{8,24},{16,0},{24,8},{1,17},{9,25},{17,1},{25,9},{2,18},{10... | collective-permute-start | bytes 49160 | tf_op jit(solution)/shard_map/ppermute | solution.py:117
  6.8 1.7 %collective-permute-done.3.refs_2_ = bf16[2,32,128]{2,1,0:T(8,128)(2,1)S(1)} collective-permute-done((bf16[2,32,128]{2,1,0:T(8,128)(2,1)S(1)}, bf16[2,32,128]{2,1,0:T(8,128)(2,1)S(1)}, u32[]{:S(2)}, u32[]{:S(2)}) %collective-permute-start.3) | collective-permute-done | bytes 16416 | tf_op jit(solution)/shard_map/ppermute | solution.py:117
  8.5 1.4 %collective-permute-done.4.refs_3_ = bf16[2,32,128]{2,1,0:T(8,128)(2,1)S(1)} collective-permute-done((bf16[2,32,128]{2,1,0:T(8,128)(2,1)S(1)}, bf16[2,32,128]{2,1,0:T(8,128)(2,1)S(1)}, u32[]{:S(2)}, u32[]{:S(2)}) %collective-permute-start.4) | collective-permute-done | bytes 16416 | tf_op jit(solution)/shard_map/ppermute | solution.py:117
  9.9 1.5 %collective-permute-start.5 = (bf16[2,128,128]{2,1,0:T(8,128)(2,1)S(1)}, bf16[2,128,128]{2,1,0:T(8,128)(2,1)S(1)}, u32[]{:S(2)}, u32[]{:S(2)}) collective-permute-start(bf16[2,128,128]{2,1,0:T(8,128)(2,1)S(1)} %shard_map.174.refs_0_.refs_9_), channel_id=1, source_target_pairs={{0,4},{4,0},{1,5},{5,1},{2,6},{6,2},{3,7},{7,3},{8,12},{12,8},{9,1... | collective-permute-start | bytes 196616 | tf_op jit(solution)/shard_map/ppermute | solution.py:107
  11.4 1.9 %shard_map.170 = (bf16[512,128]{1,0:T(8,128)(2,1)S(1)}, bf16[512,128]{1,0:T(8,128)(2,1)S(1)}, bf16[512,128]{1,0:T(8,128)(2,1)S(1)}, bf16[512,128]{1,0:T(8,128)(2...) custom-call(s32[8]{0:T(128)} %starts.1, ...), custom_call_target="tpu_custom_call" | custom-call | bytes 1591328 | tf_op jit(solution)/shard_map/pallas_call | solution.py:43
  14.1 0.8 %shard_map.172 = (bf16[512,512]{1,0:T(8,128)(2,1)S(1)}, f32[1,512]{1,0:T(1,128)S(1)}, f32[1,512]{1,0:T(1,128)S(1)}, f32[128,512]{1,0:T(8,128)S(1)}, f32[2,512]{1,0:T(2,128)S(1)}) custom-call(s32[8,512]{1,0:T(8,128)S(1)} %get-tuple-element.63.base, bf16[512,128]{1,0:T(8,128)(2,1)S(1)} %get-tuple-element.64.query.refs_8_, f32[1,512]{1,0:T(1,128)S(1)} %get-tuple-element.72.top, ...), custom_call_target="tpu_custom_call" | custom-call | flops 134217728 | bytes 1732608 | tf_op jit(solution)/shard_map/pallas_call | solution.py:43
  16.1 1.5 %collective-permute-start.7 = (f32[8,256]{1,0:T(8,128)S(1)}, f32[8,256]{1,0:T(8,128)S(1)}, u32[]{:S(2)}, u32[]{:S(2)}) collective-permute-start(f32[8,256]{1,0:T(8,128)S(1)} %get-tuple-element.81.refs_0_), channel_id=1, source_target_pairs={{0,16},{8,24},{16,0},{24,8},{1,17},{9,25},{17,1},{25,9},{2,18},{10... | collective-permute-start | bytes 24584 | tf_op jit(solution)/shard_map/ppermute | solution.py:117
  17.7 1.2 %collective-permute-done.8.refs_3_ = f32[8,256]{1,0:T(8,128)S(1)} collective-permute-done((f32[8,256]{1,0:T(8,128)S(1)}, f32[8,256]{1,0:T(8,128)S(1)}, u32[]{:S(2)}, u32[]{:S(2)}) %collective-permute-start.8) | collective-permute-done | bytes 8224 | tf_op jit(solution)/shard_map/ppermute | solution.py:117
  18.9 0.9 %collective-permute-done.7.refs_2_ = f32[8,256]{1,0:T(8,128)S(1)} collective-permute-done((f32[8,256]{1,0:T(8,128)S(1)}, f32[8,256]{1,0:T(8,128)S(1)}, u32[]{:S(2)}, u32[]{:S(2)}) %collective-permute-start.7) | collective-permute-done | bytes 8224 | tf_op jit(solution)/shard_map/ppermute | solution.py:117
  19.8 3.7 %collective-permute-start.11 = (f32[8,256]{1,0:T(8,128)S(1)}, f32[8,256]{1,0:T(8,128)S(1)}, u32[]{:S(2)}, u32[]{:S(2)}) collective-permute-start(f32[8,256]{1,0:T(8,128)S(1)} %shard_map.176.refs_0_), channel_id=1, source_target_pairs={{0,3},{1,2},{2,1},{3,0},{4,7},{5,6},{6,5},{7,4},{8,11},{9,10},{10,... | collective-permute-start | bytes 24584 | tf_op jit(solution)/shard_map/ppermute | solution.py:117
  24.2 1.1 %collective-permute-done.11.refs_3_ = f32[8,256]{1,0:T(8,128)S(1)} collective-permute-done((f32[8,256]{1,0:T(8,128)S(1)}, f32[8,256]{1,0:T(8,128)S(1)}, u32[]{:S(2)}, u32[]{:S(2)}) %collective-permute-start.11) | collective-permute-done | bytes 8224 | tf_op jit(solution)/shard_map/ppermute | solution.py:117
  25.3 2.6 %collective-permute-done.10.refs_2_ = f32[8,256]{1,0:T(8,128)S(1)} collective-permute-done((f32[8,256]{1,0:T(8,128)S(1)}, f32[8,256]{1,0:T(8,128)S(1)}, u32[]{:S(2)}, u32[]{:S(2)}) %collective-permute-start.10) | collective-permute-done | bytes 8224 | tf_op jit(solution)/shard_map/ppermute | solution.py:117
  28.6 1.1 %shard_map.178 = (bf16[2,512,128]{2,1,0:T(8,128)(2,1)S(1)}, bf16[512,512]{1,0:T(8,128)(2,1)S(1)}, f32[128,512]{1,0:T(8,128)S(1)}, f32[1,512]{1,0:T(1,128)S(1)}, f32[1,512]{1,0:T(1,128)S(1)}) custom-call(f32[8,256]{1,0:T(8,128)S(1)} %shard_map.176.refs_0_, f32[8,256]{1,0:T(8,128)S(1)} %collective-permute-done.9.refs_1_, ...), custom_call_target="tpu_custom_call" | custom-call | flops 201326592 | bytes 2402304 | tf_op jit(solution)/shard_map/pallas_call | solution.py:43
  30.4 1.4 %collective-permute-start.13 = (bf16[2,128,128]{2,1,0:T(8,128)(2,1)S(1)}, bf16[2,128,128]{2,1,0:T(8,128)(2,1)S(1)}, u32[]{:S(2)}, u32[]{:S(2)}) collective-permute-start(bf16[2,128,128]{2,1,0:T(8,128)(2,1)S(1)} %get-tuple-element.109), channel_id=1, source_target_pairs={{0,4},{4,0},{1,5},{5,1},{2,6},{6,2},{3,7},{7,3},{8,12},{12,8},{9,1... | collective-permute-start | bytes 196616 | tf_op jit(solution)/shard_map/ppermute | solution.py:107
  31.8 5.6 %collective-permute-done.13.refs_1_ = bf16[2,128,128]{2,1,0:T(8,128)(2,1)S(1)} collective-permute-done((bf16[2,128,128]{2,1,0:T(8,128)(2,1)S(1)}, bf16[2,128,128]{2,1,0:T(8,128)(2,1)S(1)}, u32[]{:S(2)}, u32[]{:S(2)}) %collective-permute-start.13) | collective-permute-done | bytes 65568 | tf_op jit(solution)/shard_map/ppermute | solution.py:107
  37.5 1.3 %collective-permute-start.15 = (bf16[2,32,128]{2,1,0:T(8,128)(2,1)S(1)}, bf16[2,32,128]{2,1,0:T(8,128)(2,1)S(1)}, u32[]{:S(2)}, u32[]{:S(2)}) collective-permute-start(bf16[2,32,128]{2,1,0:T(8,128)(2,1)S(1)} %get-tuple-element.112), channel_id=1, source_target_pairs={{0,16},{8,24},{16,0},{24,8},{1,17},{9,25},{17,1},{25,9},{2,18},{10... | collective-permute-start | bytes 49160 | tf_op jit(solution)/shard_map/ppermute | solution.py:117
  39.3 2.0 %collective-permute-done.15.refs_2_ = bf16[2,32,128]{2,1,0:T(8,128)(2,1)S(1)} collective-permute-done((bf16[2,32,128]{2,1,0:T(8,128)(2,1)S(1)}, bf16[2,32,128]{2,1,0:T(8,128)(2,1)S(1)}, u32[]{:S(2)}, u32[]{:S(2)}) %collective-permute-start.15) | collective-permute-done | bytes 16416 | tf_op jit(solution)/shard_map/ppermute | solution.py:117
  42.0 1.5 %collective-permute-start.19 = (bf16[4,2,32,128]{3,2,1,0:T(8,128)(2,1)S(1)}, bf16[4,2,32,128]{3,2,1,0:T(8,128)(2,1)S(1)}, u32[]{:S(2)}, u32[]{:S(2)}) collective-permute-start(bf16[4,2,32,128]{3,2,1,0:T(8,128)(2,1)S(1)} %shard_map.183.refs_0_), channel_id=1, source_target_pairs={{0,3},{1,2},{2,1},{3,0},{4,7},{5,6},{6,5},{7,4},{8,11},{9,10},{10,... | collective-permute-start | bytes 196616 | tf_op jit(solution)/shard_map/ppermute | solution.py:117
  44.2 2.3 %collective-permute-start.17 = (bf16[4,2,32,128]{3,2,1,0:T(8,128)(2,1)S(1)}, bf16[4,2,32,128]{3,2,1,0:T(8,128)(2,1)S(1)}, u32[]{:S(2)}, u32[]{:S(2)}) collective-permute-start(bf16[4,2,32,128]{3,2,1,0:T(8,128)(2,1)S(1)} %shard_map.183.refs_0_), channel_id=1, source_target_pairs={{0,1},{1,0},{2,3},{3,2},{4,5},{5,4},{6,7},{7,6},{8,9},{9,8},{10,11... | collective-permute-start | bytes 196616 | tf_op jit(solution)/shard_map/ppermute | solution.py:117
  46.4 1.0 %shard_map.180 = (bf16[512,128]{1,0:T(8,128)(2,1)}, bf16[512,128]{1,0:T(8,128)(2,1)}) custom-call(f32[1,512]{1,0:T(1,128)S(1)} %get-tuple-element.90.refs_11_.scale, f32[1,128]{1,0:T(1,128)S(1)} %get-tuple-element.69.cross_gain_ref.gain, f32[128,512]{1,0:T(8,128)S(1)} %get-tuple-element.86.refs_5_.attended, ...), custom_call_target="tpu_custom_call" | custom-call | flops 33554432 | bytes 920064 | tf_op jit(solution)/shard_map/pallas_call | solution.py:43
  47.5 1.9 %shard_map.179 = (f32[512,128]{1,0:T(8,128)S(1)}, f32[512,128]{1,0:T(8,128)S(1)}, bf16[512,128]{1,0:T(8,128)(2,1)}, bf16[512,128]{1,0:T(8,128)(2,1)}) custom-call(f32[128,512]{1,0:T(8,128)S(1)} %get-tuple-element.91.grad, f32[1,512]{1,0:T(1,128)S(1)} %get-tuple-element.92.scale, f32[1,512]{1,0:T(1,128)S(1)} %get-tuple-element.93.delta, ...), custom_call_target="tpu_custom_call" | custom-call | flops 335544320 | bytes 2890240 | tf_op jit(solution)/shard_map/pallas_call | solution.py:43
  49.4 1.4 %collective-permute-done.18.refs_2_ = bf16[4,2,32,128]{3,2,1,0:T(8,128)(2,1)S(1)} collective-permute-done((bf16[4,2,32,128]{3,2,1,0:T(8,128)(2,1)S(1)}, bf16[4,2,32,128]{3,2,1,0:T(8,128)(2,1)S(1)}, u32[]{:S(2)}, u32[]{:S(2)}) %collective-permute-start.18) | collective-permute-done | bytes 65568 | tf_op jit(solution)/shard_map/ppermute | solution.py:117
  (31 shorter events, 7.7 us)
Async XLA Ops:
  0.6 13.5 %collective-permute-start = (bf16[512,128]{1,0:T(8,128)(2,1)}, bf16[512,128]{1,0:T(8,128)(2,1)S(1)}, u32[]{:S(2)}, u32[]{:S(2)}) collective-permute-start(bf16[512,128]{1,0:T(8,128)(2,1)} %refs_1_.1), channel_id=1, source_target_pairs={{0,4},{4,0},{1,5},{5,1},{2,6},{6,2},{3,7},{7,3},{8,12},{12,8},{9,1... | collective-permute-start | bytes 393224 | tf_op jit(solution)/shard_map/ppermute | solution.py:107
  3.7 10.5 %collective-permute-start.1 = (bf16[512,128]{1,0:T(8,128)(2,1)}, bf16[512,128]{1,0:T(8,128)(2,1)S(1)}, u32[]{:S(2)}, u32[]{:S(2)}) collective-permute-start(bf16[512,128]{1,0:T(8,128)(2,1)} %refs_2_.1), channel_id=1, source_target_pairs={{0,4},{4,0},{1,5},{5,1},{2,6},{6,2},{3,7},{7,3},{8,12},{12,8},{9,1... | collective-permute-start | bytes 393224 | tf_op jit(solution)/shard_map/ppermute | solution.py:107
  4.6 2.2 %collective-permute-start.2 = (bf16[2,32,128]{2,1,0:T(8,128)(2,1)S(1)}, bf16[2,32,128]{2,1,0:T(8,128)(2,1)S(1)}, u32[]{:S(2)}, u32[]{:S(2)}) collective-permute-start(bf16[2,32,128]{2,1,0:T(8,128)(2,1)S(1)} %get-tuple-element.78), channel_id=1, source_target_pairs={{0,8},{8,0},{16,24},{24,16},{1,9},{9,1},{17,25},{25,17},{2,10},{10... | collective-permute-start | bytes 49160 | tf_op jit(solution)/shard_map/ppermute | solution.py:117
  4.7 3.8 %collective-permute-start.3 = (bf16[2,32,128]{2,1,0:T(8,128)(2,1)S(1)}, bf16[2,32,128]{2,1,0:T(8,128)(2,1)S(1)}, u32[]{:S(2)}, u32[]{:S(2)}) collective-permute-start(bf16[2,32,128]{2,1,0:T(8,128)(2,1)S(1)} %get-tuple-element.79), channel_id=1, source_target_pairs={{0,16},{8,24},{16,0},{24,8},{1,17},{9,25},{17,1},{25,9},{2,18},{10... | collective-permute-start | bytes 49160 | tf_op jit(solution)/shard_map/ppermute | solution.py:117
  6.8 3.2 %collective-permute-start.4 = (bf16[2,32,128]{2,1,0:T(8,128)(2,1)S(1)}, bf16[2,32,128]{2,1,0:T(8,128)(2,1)S(1)}, u32[]{:S(2)}, u32[]{:S(2)}) collective-permute-start(bf16[2,32,128]{2,1,0:T(8,128)(2,1)S(1)} %get-tuple-element.80), channel_id=1, source_target_pairs={{0,24},{8,16},{16,8},{24,0},{1,25},{9,17},{17,9},{25,1},{2,26},{10... | collective-permute-start | bytes 49160 | tf_op jit(solution)/shard_map/ppermute | solution.py:117
  9.9 5.1 %collective-permute-start.5 = (bf16[2,128,128]{2,1,0:T(8,128)(2,1)S(1)}, bf16[2,128,128]{2,1,0:T(8,128)(2,1)S(1)}, u32[]{:S(2)}, u32[]{:S(2)}) collective-permute-start(bf16[2,128,128]{2,1,0:T(8,128)(2,1)S(1)} %shard_map.174.refs_0_.refs_9_), channel_id=1, source_target_pairs={{0,4},{4,0},{1,5},{5,1},{2,6},{6,2},{3,7},{7,3},{8,12},{12,8},{9,1... | collective-permute-start | bytes 196616 | tf_op jit(solution)/shard_map/ppermute | solution.py:107
  15.7 3.1 %collective-permute-start.8 = (f32[8,256]{1,0:T(8,128)S(1)}, f32[8,256]{1,0:T(8,128)S(1)}, u32[]{:S(2)}, u32[]{:S(2)}) collective-permute-start(f32[8,256]{1,0:T(8,128)S(1)} %get-tuple-element.81.refs_0_), channel_id=1, source_target_pairs={{0,24},{8,16},{16,8},{24,0},{1,25},{9,17},{17,9},{25,1},{2,26},{10... | collective-permute-start | bytes 24584 | tf_op jit(solution)/shard_map/ppermute | solution.py:117
  16.1 3.7 %collective-permute-start.7 = (f32[8,256]{1,0:T(8,128)S(1)}, f32[8,256]{1,0:T(8,128)S(1)}, u32[]{:S(2)}, u32[]{:S(2)}) collective-permute-start(f32[8,256]{1,0:T(8,128)S(1)} %get-tuple-element.81.refs_0_), channel_id=1, source_target_pairs={{0,16},{8,24},{16,0},{24,8},{1,17},{9,25},{17,1},{25,9},{2,18},{10... | collective-permute-start | bytes 24584 | tf_op jit(solution)/shard_map/ppermute | solution.py:117
  17.6 2.2 %collective-permute-start.6 = (f32[8,256]{1,0:T(8,128)S(1)}, f32[8,256]{1,0:T(8,128)S(1)}, u32[]{:S(2)}, u32[]{:S(2)}) collective-permute-start(f32[8,256]{1,0:T(8,128)S(1)} %get-tuple-element.81.refs_0_), channel_id=1, source_target_pairs={{0,8},{8,0},{16,24},{24,16},{1,9},{9,1},{17,25},{25,17},{2,10},{10... | collective-permute-start | bytes 24584 | tf_op jit(solution)/shard_map/ppermute | solution.py:117
  19.8 5.6 %collective-permute-start.11 = (f32[8,256]{1,0:T(8,128)S(1)}, f32[8,256]{1,0:T(8,128)S(1)}, u32[]{:S(2)}, u32[]{:S(2)}) collective-permute-start(f32[8,256]{1,0:T(8,128)S(1)} %shard_map.176.refs_0_), channel_id=1, source_target_pairs={{0,3},{1,2},{2,1},{3,0},{4,7},{5,6},{6,5},{7,4},{8,11},{9,10},{10,... | collective-permute-start | bytes 24584 | tf_op jit(solution)/shard_map/ppermute | solution.py:117
  23.4 4.5 %collective-permute-start.10 = (f32[8,256]{1,0:T(8,128)S(1)}, f32[8,256]{1,0:T(8,128)S(1)}, u32[]{:S(2)}, u32[]{:S(2)}) collective-permute-start(f32[8,256]{1,0:T(8,128)S(1)} %shard_map.176.refs_0_), channel_id=1, source_target_pairs={{0,2},{1,3},{2,0},{3,1},{4,6},{5,7},{6,4},{7,5},{8,10},{9,11},{10,... | collective-permute-start | bytes 24584 | tf_op jit(solution)/shard_map/ppermute | solution.py:117
  23.4 4.5 %collective-permute-start.9 = (f32[8,256]{1,0:T(8,128)S(1)}, f32[8,256]{1,0:T(8,128)S(1)}, u32[]{:S(2)}, u32[]{:S(2)}) collective-permute-start(f32[8,256]{1,0:T(8,128)S(1)} %shard_map.176.refs_0_), channel_id=1, source_target_pairs={{0,1},{1,0},{2,3},{3,2},{4,5},{5,4},{6,7},{7,6},{8,9},{9,8},{10,11... | collective-permute-start | bytes 24584 | tf_op jit(solution)/shard_map/ppermute | solution.py:117
  29.7 21.9 %collective-permute-start.12 = (bf16[2,512,128]{2,1,0:T(8,128)(2,1)S(1)}, bf16[2,512,128]{2,1,0:T(8,128)(2,1)S(1)}, u32[]{:S(2)}, u32[]{:S(2)}) collective-permute-start(bf16[2,512,128]{2,1,0:T(8,128)(2,1)S(1)} %get-tuple-element.104), channel_id=1, source_target_pairs={{0,4},{4,0},{1,5},{5,1},{2,6},{6,2},{3,7},{7,3},{8,12},{12,8},{9,1... | collective-permute-start | bytes 786440 | tf_op jit(solution)/shard_map/ppermute | solution.py:107
  30.4 7.0 %collective-permute-start.13 = (bf16[2,128,128]{2,1,0:T(8,128)(2,1)S(1)}, bf16[2,128,128]{2,1,0:T(8,128)(2,1)S(1)}, u32[]{:S(2)}, u32[]{:S(2)}) collective-permute-start(bf16[2,128,128]{2,1,0:T(8,128)(2,1)S(1)} %get-tuple-element.109), channel_id=1, source_target_pairs={{0,4},{4,0},{1,5},{5,1},{2,6},{6,2},{3,7},{7,3},{8,12},{12,8},{9,1... | collective-permute-start | bytes 196616 | tf_op jit(solution)/shard_map/ppermute | solution.py:107
  37.4 1.9 %collective-permute-start.14 = (bf16[2,32,128]{2,1,0:T(8,128)(2,1)S(1)}, bf16[2,32,128]{2,1,0:T(8,128)(2,1)S(1)}, u32[]{:S(2)}, u32[]{:S(2)}) collective-permute-start(bf16[2,32,128]{2,1,0:T(8,128)(2,1)S(1)} %get-tuple-element.111), channel_id=1, source_target_pairs={{0,8},{8,0},{16,24},{24,16},{1,9},{9,1},{17,25},{25,17},{2,10},{10... | collective-permute-start | bytes 49160 | tf_op jit(solution)/shard_map/ppermute | solution.py:117
  37.5 3.8 %collective-permute-start.15 = (bf16[2,32,128]{2,1,0:T(8,128)(2,1)S(1)}, bf16[2,32,128]{2,1,0:T(8,128)(2,1)S(1)}, u32[]{:S(2)}, u32[]{:S(2)}) collective-permute-start(bf16[2,32,128]{2,1,0:T(8,128)(2,1)S(1)} %get-tuple-element.112), channel_id=1, source_target_pairs={{0,16},{8,24},{16,0},{24,8},{1,17},{9,25},{17,1},{25,9},{2,18},{10... | collective-permute-start | bytes 49160 | tf_op jit(solution)/shard_map/ppermute | solution.py:117
  38.8 3.2 %collective-permute-start.16 = (bf16[2,32,128]{2,1,0:T(8,128)(2,1)S(1)}, bf16[2,32,128]{2,1,0:T(8,128)(2,1)S(1)}, u32[]{:S(2)}, u32[]{:S(2)}) collective-permute-start(bf16[2,32,128]{2,1,0:T(8,128)(2,1)S(1)} %get-tuple-element.113), channel_id=1, source_target_pairs={{0,24},{8,16},{16,8},{24,0},{1,25},{9,17},{17,9},{25,1},{2,26},{10... | collective-permute-start | bytes 49160 | tf_op jit(solution)/shard_map/ppermute | solution.py:117
  42.0 7.4 %collective-permute-start.19 = (bf16[4,2,32,128]{3,2,1,0:T(8,128)(2,1)S(1)}, bf16[4,2,32,128]{3,2,1,0:T(8,128)(2,1)S(1)}, u32[]{:S(2)}, u32[]{:S(2)}) collective-permute-start(bf16[4,2,32,128]{3,2,1,0:T(8,128)(2,1)S(1)} %shard_map.183.refs_0_), channel_id=1, source_target_pairs={{0,3},{1,2},{2,1},{3,0},{4,7},{5,6},{6,5},{7,4},{8,11},{9,10},{10,... | collective-permute-start | bytes 196616 | tf_op jit(solution)/shard_map/ppermute | solution.py:117
  43.5 7.3 %collective-permute-start.18 = (bf16[4,2,32,128]{3,2,1,0:T(8,128)(2,1)S(1)}, bf16[4,2,32,128]{3,2,1,0:T(8,128)(2,1)S(1)}, u32[]{:S(2)}, u32[]{:S(2)}) collective-permute-start(bf16[4,2,32,128]{3,2,1,0:T(8,128)(2,1)S(1)} %shard_map.183.refs_0_), channel_id=1, source_target_pairs={{0,2},{1,3},{2,0},{3,1},{4,6},{5,7},{6,4},{7,5},{8,10},{9,11},{10,... | collective-permute-start | bytes 196616 | tf_op jit(solution)/shard_map/ppermute | solution.py:117
  44.2 6.6 %collective-permute-start.17 = (bf16[4,2,32,128]{3,2,1,0:T(8,128)(2,1)S(1)}, bf16[4,2,32,128]{3,2,1,0:T(8,128)(2,1)S(1)}, u32[]{:S(2)}, u32[]{:S(2)}) collective-permute-start(bf16[4,2,32,128]{3,2,1,0:T(8,128)(2,1)S(1)} %shard_map.183.refs_0_), channel_id=1, source_target_pairs={{0,1},{1,0},{2,3},{3,2},{4,5},{5,4},{6,7},{7,6},{8,9},{9,8},{10,11... | collective-permute-start | bytes 196616 | tf_op jit(solution)/shard_map/ppermute | solution.py:117
where the time goes:
time: 52.5 us; the launch traced here: 52.3 us
  starting transfers between devices  21.6 us (41%)
  waiting for transfers between devices  18.7 us (36%)
  Pallas kernels  11.3 us (22%)
  between operations  0.75 us (1%)
    ppermute x15, starting transfers between devices, swapped(): return lax.ppermute(value, axis, [(at, at ^ by) for at in range(count)])  14.9 us
    ppermute x15, waiting for transfers between devices, swapped(): return lax.ppermute(value, axis, [(at, at ^ by) for at in range(count)])  13.1 us
    pallas_call x15, Pallas kernels, call(): pl.pallas_call(body, out_shape=shapes, in_specs=[SMEM] * smem + [space] *...  11.3 us
    ppermute x5, starting transfers between devices, shifted(): lax.ppermute(value, axis, [(at, (at + by) % count) for at in range(count)])  6.69 us
    ppermute x5, waiting for transfers between devices, shifted(): lax.ppermute(value, axis, [(at, (at + by) % count) for at in range(count)])  5.59 us
  transfers between devices with their start and end apart: 20, of which 10 were waited for; matrix products, arithmetic and copies ran while one was open for 0% of the time, Pallas kernels for 16%

commit v1 on v0

--- a/solution.py
+++ b/solution.py
@@ -72,10 +72,10 @@
     return jnp.concatenate(parts, axis=1)
 
 
-def fold_block(key, value, queries, running, store, masks, held, scaling):
+def fold_scores(key, queries, running, store, masks, held, scaling):
     rows, step = key.shape[0], 128
     step = min(step, rows)
-    top, total, weighted = running
+    top, total = running
     block_top = top
     for at in range(0, rows, step):
         scores = dot_nt(key[at : at + step, :], queries) * scaling
@@ -92,11 +92,9 @@
         part = jnp.sum(raised, axis=0, keepdims=True)
         block_total = part if block_total is None else block_total + part
         store[at : at + step, :] = raised.astype(BF16)
-    product = dot_tn(value[...], store[...])
-    if top is None:
-        return block_top, block_total, product
-    shrink = jnp.exp(top - block_top)
-    return block_top, total * shrink + block_total, weighted * shrink + product
+    if top is not None:
+        block_total = total * jnp.exp(top - block_top) + block_total
+    return block_top, block_total
 
 
 def solution(mesh):
@@ -122,6 +120,7 @@
 
     def over_tensors(value, by):
         return swapped(value, "tp", tensors, by)
+
 
     def per_device(
         self_query,
@@ -161,19 +160,19 @@
                 copy.wait()
 
         def load_memory(key_ref, value_ref, *refs):
-            outs, semaphores = refs[:-1], refs[-1]
+            out, semaphores = refs
             section, tensor = lax.axis_index("sec"), lax.axis_index("tp")
             moves = []
-            for by, out in enumerate(outs):
+            for by in range(sections):
                 head = paired(section, by, sections) * tensors + tensor
                 at = pl.ds(pl.multiple_of(head * columns, columns), columns)
-                moves += [(key_ref.at[:, at], out.at[0]), (value_ref.at[:, at], out.at[1])]
+                moves += [(key_ref.at[:, at], out.at[by, 0]), (value_ref.at[:, at], out.at[by, 1])]
             copy_all(moves, semaphores)
 
-        pieces = call(
+        (pieces,) = call(
             load_memory,
             [memory_key, memory_value],
-            [((2, rows, columns), BF16)] * sections,
+            [((sections, 2, rows, columns), BF16)],
             scratch=[pltpu.SemaphoreType.DMA((2 * sections,))],
             loads=True,
         )
@@ -189,11 +188,14 @@
             cross_gain.reshape(1, columns),
         ]
 
-        def load_rows(starts, *refs):
+        def load_rows(start_ref, *refs):
             count = len(plain)
-            bases, semaphores = refs[-2:]
+            bases, starts, start_semaphore, semaphores = refs[-4:]
+            first_copy = pltpu.make_async_copy(start_ref, starts, start_semaphore)
+            first_copy.start()
 
             def positions():
+                first_copy.wait()
                 context = lax.axis_index("ctx")
                 for by in range(contexts):
                     source = lax.rem(context - by + contexts, contexts)
@@ -211,23 +213,33 @@
             load_rows,
             [block_start] + plain,
             [(entry.shape, entry.dtype) for entry in plain] + [((4 * contexts, frames), jnp.int32)],
-            scratch=[pltpu.SemaphoreType.DMA((len(plain),))],
-            smem=1,
+            scratch=[
+                pltpu.SMEM(block_start.shape, jnp.int32),
+                pltpu.SemaphoreType.DMA,
+                pltpu.SemaphoreType.DMA((len(plain),)),
+            ],
             loads=True,
         )
         self_query, self_key, self_value, self_grad, cross_query, cross_grad, self_gain, cross_gain, bases = results
 
-        arrived = [pieces[0]] + [over_sections(pieces[by], by) for by in range(1, sections)]
+        blocks_in = [pieces] + [shifted(pieces, "ctx", contexts, by) for by in range(1, contexts)]
+
+        def regroup(*refs):
+            ins, outs = refs[:contexts], refs[contexts:]
+            for by, out in enumerate(outs):
+                for at, ref in enumerate(ins):
+                    out[at] = ref[by]
+
+        packs = call(regroup, blocks_in, [((contexts, 2, rows, columns), BF16)] * sections)
+        arrived = [packs[0]] + [over_sections(packs[by], by) for by in range(1, sections)]
 
         def gather(*refs):
-            out = refs[-1]
-            for at, ref in enumerate(refs[:-1]):
-                out[:, at * rows : (at + 1) * rows, :] = ref[...]
-
-        (own_memory,) = call(gather, arrived, [((2, group, columns), BF16)])
-        memories = [own_memory] + [
-            shifted(own_memory, "ctx", contexts, by) for by in range(1, contexts)
-        ]
+            ins, outs = refs[:sections], refs[sections:]
+            for at, out in enumerate(outs):
+                for by, ref in enumerate(ins):
+                    out[:, by * rows : (by + 1) * rows, :] = ref[at]
+
+        memories = call(gather, arrived, [((2, group, columns), BF16)] * contexts)
 
         def first_block(
             base,
@@ -250,9 +262,10 @@
                 lambda at: base[at // quarter : at // quarter + 1, :] + at % quarter,
                 row_positions(base, quarter),
             )
-            top[...], total[...], weighted[...] = fold_block(
-                key, value, query[...], (None, None, None), store, masks, held, scaling
+            top[...], total[...] = fold_scores(
+                key, query[...], (None, None), store, masks, held, scaling
             )
+            weighted[...] = dot_tn(value[...], store[...])
             lifted[...] = (gain[...] * grad[...].astype(F32)).T
             cross_lifted_ref[...] = (cross_gain_ref[...] * cross_grad_ref[...].astype(F32)).T
 
@@ -279,12 +292,11 @@
                 jnp.sum(lifted * attended, axis=0, keepdims=True),
             )
 
-        def other_blocks(base, query, top, total, weighted, lifted, *refs):
-            keys, values = refs[:others], refs[others : 2 * others]
-            stores = refs[2 * others : 3 * others]
-            first_weight, weight, attended_ref, stats, held = refs[3 * others :]
+        def other_scores(base, query, top, total, *refs):
+            keys, stores = refs[:others], refs[others : 2 * others]
+            first_weight, weight, held = refs[2 * others :]
             positions = row_positions(base, quarter)
-            running = (top[...], total[...], weighted[...])
+            running = (top[...], total[...])
             tops = [top[...]]
             for by in range(others):
                 first = 4 * (by + 1)
@@ -293,85 +305,86 @@
                     + at % quarter,
                     positions,
                 )
-                running = fold_block(
-                    keys[by], values[by], query[...], running, stores[by], masks, held, scaling
-                )
+                running = fold_scores(keys[by], query[...], running, stores[by], masks, held, scaling)
                 tops.append(running[0])
             last = 1.0 / running[1]
             first_weight[...] = jnp.exp(tops[0] - running[0]) * last
             for by in range(others):
                 weight[by : by + 1, :] = jnp.exp(tops[by + 1] - running[0]) * last
-            attended = running[2] * last
+
+        results = call(
+            other_scores,
+            [bases, self_query, first_top, first_total] + other_keys,
+            [((frames, frames), BF16)] * others + [(line, F32), ((others, frames), F32)],
+            flops=frames * unit * others,
+            scratch=[pltpu.VMEM((frames, frames), F32)],
+        )
+        other_stores, (first_weight, other_weight) = results[:others], results[others:]
+
+        def cross_forward(query, lifted, *refs):
+            blocks, stores = refs[:contexts], refs[contexts : 2 * contexts]
+            weight, attended_ref, stats, held = refs[2 * contexts :]
+            running = (None, None)
+            tops = []
+            for at in range(contexts):
+                running = fold_scores(blocks[at].at[0], query[...], running, stores[at], None, held, scaling)
+                tops.append(running[0])
+            last = 1.0 / running[1]
+            attended = None
+            for at in range(contexts):
+                factor = jnp.exp(tops[at] - running[0]) * last
+                weight[at : at + 1, :] = factor
+                part = dot_tn(blocks[at][1], stores[at][...]) * factor
+                attended = part if attended is None else attended + part
             attended_ref[...] = attended
             stats[0:1, :], stats[1:2, :] = statistics(attended, lifted[...])
 
         results = call(
-            other_blocks,
-            [bases, self_query, first_top, first_total, first_weighted, self_lifted]
-            + other_keys
-            + other_values,
-            [((frames, frames), BF16)] * others
-            + [(line, F32), ((others, frames), F32), (tall, F32), ((2, frames), F32)],
-            flops=2 * frames * unit * others,
-            scratch=[pltpu.VMEM((frames, frames), F32)],
-        )
-        other_stores = results[:others]
-        first_weight, other_weight, self_attended, self_stats = results[others:]
-
-        half = frames // 2
-
-        def cross_forward(query, lifted, self_stats_ref, *refs):
-            blocks, stores = refs[:contexts], refs[contexts : 2 * contexts]
-            weight, attended_ref, stats, packed, held = refs[2 * contexts :]
-            running = (None, None, None)
-            tops = []
-            for at in range(contexts):
-                running = fold_block(
-                    blocks[at].at[0], blocks[at].at[1], query[...], running, stores[at], None, held, scaling
-                )
-                tops.append(running[0])
-            last = 1.0 / running[1]
-            for at in range(contexts):
-                weight[at : at + 1, :] = jnp.exp(tops[at] - running[0]) * last
-            attended = running[2] * last
-            attended_ref[...] = attended
-            squares, slopes = statistics(attended, lifted[...])
-            stats[0:1, :], stats[1:2, :] = squares, slopes
-            lines = [self_stats_ref[0:1, :], self_stats_ref[1:2, :], squares, slopes]
-            halves = [entry[:, at : at + half] for entry in lines for at in (0, half)]
-            tile = jnp.concatenate(halves, axis=0)
-            packed[...] = tile
-
-        results = call(
             cross_forward,
-            [cross_query, cross_lifted, self_stats] + memories,
+            [cross_query, cross_lifted] + memories,
             [((group, frames), BF16)] * contexts
             + [
                 ((contexts, frames), F32),
                 (tall, F32),
                 ((2, frames), F32),
-                ((8, half), F32),
             ],
             flops=2 * group * contexts * unit,
             scratch=[pltpu.VMEM((group, frames), F32)],
         )
         cross_stores = results[:contexts]
-        cross_weight, cross_attended, cross_stats, packed = results[contexts:]
-
-        def add_all(*refs):
-            total = refs[0][...]
-            for ref in refs[1:-1]:
-                total = total + ref[...]
-            refs[-1][...] = total
-
-        near = [packed] + [over_sections(packed, by) for by in range(1, sections)]
-        (partial,) = call(add_all, near, [((8, half), F32)])
-        received = [partial] + [over_tensors(partial, by) for by in range(1, tensors)]
+        cross_weight, cross_attended, cross_stats = results[contexts:]
+
+        half = frames // 2
+
+        def other_values_seen(weighted, first_weight_ref, weight, lifted, cross_stats_ref, *refs):
+            values, stores = refs[:others], refs[others : 2 * others]
+            attended_ref, stats, packed = refs[2 * others :]
+            attended = weighted[...] * first_weight_ref[...]
+            for by in range(others):
+                attended = attended + dot_tn(values[by][...], stores[by][...]) * weight[by : by + 1, :]
+            attended_ref[...] = attended
+            squares, slopes = statistics(attended, lifted[...])
+            stats[0:1, :], stats[1:2, :] = squares, slopes
+            lines = [squares, slopes, cross_stats_ref[0:1, :], cross_stats_ref[1:2, :]]
+            halves = [entry[:, at : at + half] for entry in lines for at in (0, half)]
+            tile = jnp.concatenate(halves, axis=0)
+            for at in range(peers):
+                packed[at] = tile
+
+        self_attended, self_stats, packed = call(
+            other_values_seen,
+            [first_weighted, first_weight, other_weight, self_lifted, cross_stats] + other_values + other_stores,
+            [(tall, F32), ((2, frames), F32), ((peers, 8, half), F32)],
+            flops=frames * unit * others,
+        )
+
+
+        received = [lax.all_to_all(packed, ("sec", "tp"), split_axis=0, concat_axis=0, tiled=True)]
 
         def norm_terms(received_ref, stats, attended, lifted, at):
-            sums = received_ref[0][...]
-            for entry in received_ref[1:]:
-                sums = sums + entry[...]
+            sums = received_ref[0][0]
+            for source in range(1, peers):
+                sums = sums + received_ref[0][source]
             joined = [
                 jnp.concatenate([sums[2 * pick : 2 * pick + 1], sums[2 * pick + 1 : 2 * pick + 2]], axis=1)
                 for pick in (2 * at, 2 * at + 1)
@@ -394,52 +407,66 @@
                 key_grad(at, step, dot_nn(slope, query) * scaling)
                 value_grad(at, step, dot_nn(probs, grad_wide))
 
+        def memory_grads(block, store, factor, delta, grad, query, out, slopes):
+            grad_wide = (grad * factor).T.astype(BF16)
+
+            def key_grad(first, count, value):
+                out[0, first : first + count, :] = value.astype(out.dtype)
+
+            def value_grad(first, count, value):
+                out[1, first : first + count, :] = value.astype(out.dtype)
+
+            block_grads(
+                key_grad,
+                value_grad,
+                block.at[1],
+                store,
+                factor,
+                delta,
+                grad.astype(BF16),
+                grad_wide,
+                query[...],
+                slopes,
+            )
+
         def cross_backward(*refs):
-            received_ref, (stats, attended, lifted, weight, query) = refs[:tensors], refs[tensors : tensors + 5]
-            refs = refs[tensors + 5 :]
-            blocks, stores = refs[:contexts], refs[contexts : 2 * contexts]
-            sums, slopes, scale_ref = refs[2 * contexts : 3 * contexts], refs[3 * contexts : 4 * contexts], refs[-1]
+            received_ref, (stats, attended, lifted, weight, query) = refs[:1], refs[1:6]
+            refs = refs[6:]
+            blocks, stores = refs[:others], refs[others : 2 * others]
+            sums, slopes = refs[2 * others : 3 * others], refs[3 * others : 4 * others]
+            scale_ref, delta_ref, grad_ref = refs[4 * others :]
             scale, delta, grad = norm_terms(received_ref, stats, attended, lifted, 1)
-            scale_ref[...] = scale
-            grad_tall = grad.astype(BF16)
-            for at in range(contexts):
-                line_weight = weight[at : at + 1, :]
-                grad_wide = (grad * line_weight).T.astype(BF16)
-
-                def key_grad(first, count, value, out=sums[at]):
-                    out[0, first : first + count, :] = value.astype(out.dtype)
-
-                def value_grad(first, count, value, out=sums[at]):
-                    out[1, first : first + count, :] = value.astype(out.dtype)
-
-                block_grads(
-                    key_grad,
-                    value_grad,
-                    blocks[at].at[1],
-                    stores[at],
-                    line_weight,
-                    delta,
-                    grad_tall,
-                    grad_wide,
-                    query[...],
-                    slopes[at],
-                )
+            scale_ref[...], delta_ref[...], grad_ref[...] = scale, delta, grad
+            for by in range(others):
+                factor = weight[by + 1 : by + 2, :]
+                memory_grads(blocks[by], stores[by], factor, delta, grad, query, sums[by], slopes[by])
 
         results = call(
             cross_backward,
             received
             + [cross_stats, cross_attended, cross_lifted, cross_weight, cross_query]
-            + memories
-            + list(cross_stores),
-            [((2, group, columns), F32)]
-            + [((2, group, columns), BF16)] * others
-            + [((group, frames), BF16)] * contexts
-            + [(line, F32)],
-            flops=3 * group * contexts * unit,
-        )
-        memory_sums, cross_slopes, cross_scale = results[:contexts], results[contexts:-1], results[-1]
-
-        returned = [shifted(memory_sums[by], "ctx", contexts, -by) for by in range(1, contexts)]
+            + memories[1:]
+            + cross_stores[1:],
+            [((2, group, columns), BF16)] * others
+            + [((group, frames), BF16)] * others
+            + [(line, F32), (line, F32), (tall, F32)],
+            flops=3 * group * others * unit,
+        )
+        away_sums, away_slopes = results[:others], results[others : 2 * others]
+        cross_scale, cross_delta, cross_attended_grad = results[2 * others :]
+
+        def cross_own(delta, grad, weight, query, block, store, out, slopes):
+            memory_grads(block, store, weight[0:1, :], delta[...], grad[...], query, out, slopes)
+
+        own_sums, own_slopes_cross = call(
+            cross_own,
+            [cross_delta, cross_attended_grad, cross_weight, cross_query, memories[0], cross_stores[0]],
+            [((2, group, columns), F32), ((group, frames), BF16)],
+            flops=3 * group * unit,
+        )
+        cross_slopes = [own_slopes_cross] + away_slopes
+
+        returned = [shifted(away_sums[by], "ctx", contexts, -(by + 1)) for by in range(others)]
 
         def add_up(*refs):
             own, extra, outs = refs[0], refs[1 : 1 + others], refs[1 + others :]
@@ -450,7 +477,7 @@
                     total = total + entry[:, part, :].astype(F32)
                 out[...] = total.astype(BF16)
 
-        parts = call(add_up, [memory_sums[0]] + returned, [((2, rows, columns), BF16)] * sections)
+        parts = call(add_up, [own_sums] + returned, [((2, rows, columns), BF16)] * sections)
         back = [parts[0]] + [over_sections(parts[by], by, back=True) for by in range(1, sections)]
 
         def by_section(*refs):
@@ -478,8 +505,8 @@
         )
 
         def other_backward(*refs):
-            received_ref, (stats, attended, lifted, weight, query) = refs[:tensors], refs[tensors : tensors + 5]
-            refs = refs[tensors + 5 :]
+            received_ref, (stats, attended, lifted, weight, query) = refs[:1], refs[1:6]
+            refs = refs[6:]
             values, stores = refs[:others], refs[others : 2 * others]
             pairs_out, slopes = refs[2 * others : 3 * others], refs[3 * others : 4 * others]
             grad_ref, scale_ref, delta_ref = refs[4 * others :]

time: 52.5 us -> 56.4 us (1.074)
  blocking collectives: 0 us -> 12.4 us
  starting transfers between devices: 21.6 us -> 15.8 us
  waiting for transfers between devices: 18.7 us -> 16.6 us
  Pallas kernels: 11.3 us -> 10.6 us
    all_to_all x0 -> x1, blocking collectives: none -> 12.4 us  [per_device(): lax.all_to_all(packed, ('sec', 'tp'), split_axis=0, concat_axis=0, tiled=...]
    ppermute x15 -> x9, waiting for transfers between devices: 13.1 us -> 4.28 us  [swapped(): return lax.ppermute(value, axis, [(at, at ^ by) for at in range(count)])]
    ppermute x5, waiting for transfers between devices: 5.59 us -> 12.3 us  [shifted(): lax.ppermute(value, axis, [(at, (at + by) % count) for at in range(count)])]
    ppermute x15 -> x9, starting transfers between devices: 14.9 us -> 8.59 us  [swapped(): return lax.ppermute(value, axis, [(at, at ^ by) for at in range(count)])]
    pallas_call x15 -> x17, Pallas kernels: 11.3 us -> 10.6 us  [call(): pl.pallas_call(body, out_shape=shapes, in_specs=[SMEM] * smem + [space] *...]
  transfers between devices with their start and end apart: 20 -> 14, of which waited for: 10 -> 6; matrix products, arithmetic and copies ran while one was open for 0% -> 0% of each run, Pallas kernels for 16% -> 14%
where the time goes in v1:
time: 56.4 us; the launch traced here: 56.2 us
  waiting for transfers between devices  16.6 us (29%)
  starting transfers between devices  15.8 us (28%)
  blocking collectives  12.4 us (22%)
  Pallas kernels  10.6 us (19%)
  between operations  0.75 us (1%)
    all_to_all x1, blocking collectives, per_device(): lax.all_to_all(packed, ('sec', 'tp'), split_axis=0, concat_axis=0, tiled=...  12.4 us
    ppermute x5, waiting for transfers between devices, shifted(): lax.ppermute(value, axis, [(at, (at + by) % count) for at in range(count)])  12.3 us
    pallas_call x17, Pallas kernels, call(): pl.pallas_call(body, out_shape=shapes, in_specs=[SMEM] * smem + [space] *...  10.6 us
    ppermute x9, starting transfers between devices, swapped(): return lax.ppermute(value, axis, [(at, at ^ by) for at in range(count)])  8.59 us
    ppermute x5, starting transfers between devices, shifted(): lax.ppermute(value, axis, [(at, (at + by) % count) for at in range(count)])  7.21 us
    ppermute x9, waiting for transfers between devices, swapped(): return lax.ppermute(value, axis, [(at, at ^ by) for at in range(count)])  4.28 us
  transfers between devices with their start and end apart: 14, of which 6 were waited for; matrix products, arithmetic and copies ran while one was open for 0% of the time, Pallas kernels for 14%

profile of v1, /device:TPU:0, one launch (start us, length us, event | category | flops | bytes accessed | tf_op | source)
XLA Modules:
  0.0 56.2 jit_solution(5902151236188767537)
XLA Ops:
  0.6 3.0 %collective-permute-start = (bf16[512,128]{1,0:T(8,128)(2,1)}, bf16[512,128]{1,0:T(8,128)(2,1)S(1)}, u32[]{:S(2)}, u32[]{:S(2)}) collective-permute-start(bf16[512,128]{1,0:T(8,128)(2,1)} %refs_1_.1), channel_id=1, source_target_pairs={{0,4},{4,0},{1,5},{5,1},{2,6},{6,2},{3,7},{7,3},{8,12},{12,8},{9,1... | collective-permute-start | bytes 393224 | tf_op jit(solution)/shard_map/ppermute | solution.py:105
  3.7 0.9 %shard_map.173.refs_0_ = bf16[4,2,32,128]{3,2,1,0:T(8,128)(2,1)S(1)} custom-call(bf16[32,2048]{1,0:T(8,128)(2,1)} %key_ref.1, bf16[32,2048]{1,0:T(8,128)(2,1)} %value_ref.1), custom_call_target="tpu_custom_call" | custom-call | bytes 327680 | tf_op jit(solution)/shard_map/pallas_call | solution.py:43
  4.6 2.0 %collective-permute-start.1 = (bf16[4,2,32,128]{3,2,1,0:T(8,128)(2,1)S(1)}, bf16[4,2,32,128]{3,2,1,0:T(8,128)(2,1)S(1)}, u32[]{:S(2)}, u32[]{:S(2)}) collective-permute-start(bf16[4,2,32,128]{3,2,1,0:T(8,128)(2,1)S(1)} %shard_map.173.refs_0_), channel_id=1, source_target_pairs={{0,4},{4,0},{1,5},{5,1},{2,6},{6,2},{3,7},{7,3},{8,12},{12,8},{9,1... | collective-permute-start | bytes 196616 | tf_op jit(solution)/shard_map/ppermute | solution.py:105
  6.6 4.9 %collective-permute-done.1.refs_1_ = bf16[4,2,32,128]{3,2,1,0:T(8,128)(2,1)S(1)} collective-permute-done((bf16[4,2,32,128]{3,2,1,0:T(8,128)(2,1)S(1)}, bf16[4,2,32,128]{3,2,1,0:T(8,128)(2,1)S(1)}, u32[]{:S(2)}, u32[]{:S(2)}) %collective-permute-start.1) | collective-permute-done | bytes 65568 | tf_op jit(solution)/shard_map/ppermute | solution.py:105
  11.7 1.8 %collective-permute-start.3 = (bf16[2,2,32,128]{3,2,1,0:T(8,128)(2,1)S(1)}, bf16[2,2,32,128]{3,2,1,0:T(8,128)(2,1)S(1)}, u32[]{:S(2)}, u32[]{:S(2)}) collective-permute-start(bf16[2,2,32,128]{3,2,1,0:T(8,128)(2,1)S(1)} %get-tuple-element.84), channel_id=1, source_target_pairs={{0,16},{8,24},{16,0},{24,8},{1,17},{9,25},{17,1},{25,9},{2,18},{10... | collective-permute-start | bytes 98312 | tf_op jit(solution)/shard_map/ppermute | solution.py:115
  13.6 1.3 %shard_map.170 = (bf16[512,128]{1,0:T(8,128)(2,1)S(1)}, bf16[512,128]{1,0:T(8,128)(2,1)S(1)}, bf16[512,128]{1,0:T(8,128)(2,1)S(1)}, bf16[512,128]{1,0:T(8,128)(2...) custom-call(s32[8]{0:T(128)} %start_ref.1, ...), custom_call_target="tpu_custom_call" | custom-call | bytes 1591328 | tf_op jit(solution)/shard_map/pallas_call | solution.py:43
  14.8 0.8 %shard_map.171 = (bf16[512,512]{1,0:T(8,128)(2,1)S(1)}, f32[1,512]{1,0:T(1,128)S(1)}, f32[1,512]{1,0:T(1,128)S(1)}, f32[128,512]{1,0:T(8,128)S(1)}, f32[128,512]{1,0:T(8,128)S(1)}, /*index=5*/f32[128,512]{1,0:T(8,128)S(1)}) custom-call(s32[8,512]{1,0:T(8,128)S(1)} %get-tuple-element.66.base, bf16[512,128]{1,0:T(8,128)(2,1)S(1)} %get-tuple-element.67.query.refs_5_, ...), custom_call_target="tpu_custom_call" | custom-call | flops 134217728 | bytes 1987584 | tf_op jit(solution)/shard_map/pallas_call | solution.py:43
  15.7 1.2 %collective-permute-done.4.refs_3_ = bf16[2,2,32,128]{3,2,1,0:T(8,128)(2,1)S(1)} collective-permute-done((bf16[2,2,32,128]{3,2,1,0:T(8,128)(2,1)S(1)}, bf16[2,2,32,128]{3,2,1,0:T(8,128)(2,1)S(1)}, u32[]{:S(2)}, u32[]{:S(2)}) %collective-permute-start.4) | collective-permute-done | bytes 32800 | tf_op jit(solution)/shard_map/ppermute | solution.py:115
  18.3 12.4 %all_to_all.5.refs_0_ = f32[16,8,256]{2,1,0:T(8,128)S(1)} all-to-all(f32[16,8,256]{2,1,0:T(8,128)S(1)} %get-tuple-element.90), channel_id=1, replica_groups=mesh['sec'=4,'ctx'=2,'tp'=4] {'sec','tp'}, dimensions={0} | all-to-all | bytes 262144 | tf_op jit(solution)/shard_map/all_to_all | solution.py:382
  31.2 1.1 %shard_map.179 = (bf16[2,512,128]{2,1,0:T(8,128)(2,1)S(1)}, bf16[512,512]{1,0:T(8,128)(2,1)S(1)}, f32[128,512]{1,0:T(8,128)S(1)}, f32[1,512]{1,0:T(1,128)S(1)}, f32[1,512]{1,0:T(1,128)S(1)}) custom-call(f32[16,8,256]{2,1,0:T(8,128)S(1)} %all_to_all.5.refs_0_, f32[2,512]{1,0:T(2,128)S(1)} %get-tuple-element.91.refs_1_, ...), custom_call_target="tpu_custom_call" | custom-call | flops 201326592 | bytes 2500608 | tf_op jit(solution)/shard_map/pallas_call | solution.py:43
  32.3 1.5 %collective-permute-start.6 = (bf16[2,512,128]{2,1,0:T(8,128)(2,1)S(1)}, bf16[2,512,128]{2,1,0:T(8,128)(2,1)S(1)}, u32[]{:S(2)}, u32[]{:S(2)}) collective-permute-start(bf16[2,512,128]{2,1,0:T(8,128)(2,1)S(1)} %get-tuple-element.112), channel_id=1, source_target_pairs={{0,4},{4,0},{1,5},{5,1},{2,6},{6,2},{3,7},{7,3},{8,12},{12,8},{9,1... | collective-permute-start | bytes 786440 | tf_op jit(solution)/shard_map/ppermute | solution.py:105
  34.7 7.3 %collective-permute-done.7.refs_1_ = bf16[2,128,128]{2,1,0:T(8,128)(2,1)S(1)} collective-permute-done((bf16[2,128,128]{2,1,0:T(8,128)(2,1)S(1)}, bf16[2,128,128]{2,1,0:T(8,128)(2,1)S(1)}, u32[]{:S(2)}, u32[]{:S(2)}) %collective-permute-start.7) | collective-permute-done | bytes 65568 | tf_op jit(solution)/shard_map/ppermute | solution.py:105
  42.2 0.7 %collective-permute-start.8 = (bf16[2,32,128]{2,1,0:T(8,128)(2,1)S(1)}, bf16[2,32,128]{2,1,0:T(8,128)(2,1)S(1)}, u32[]{:S(2)}, u32[]{:S(2)}) collective-permute-start(bf16[2,32,128]{2,1,0:T(8,128)(2,1)S(1)} %get-tuple-element.119), channel_id=1, source_target_pairs={{0,8},{8,0},{16,24},{24,16},{1,9},{9,1},{17,25},{25,17},{2,10},{10... | collective-permute-start | bytes 49160 | tf_op jit(solution)/shard_map/ppermute | solution.py:115
  42.9 1.4 %collective-permute-start.9 = (bf16[2,32,128]{2,1,0:T(8,128)(2,1)S(1)}, bf16[2,32,128]{2,1,0:T(8,128)(2,1)S(1)}, u32[]{:S(2)}, u32[]{:S(2)}) collective-permute-start(bf16[2,32,128]{2,1,0:T(8,128)(2,1)S(1)} %get-tuple-element.120), channel_id=1, source_target_pairs={{0,16},{8,24},{16,0},{24,8},{1,17},{9,25},{17,1},{25,9},{2,18},{10... | collective-permute-start | bytes 49160 | tf_op jit(solution)/shard_map/ppermute | solution.py:115
  44.3 1.0 %collective-permute-done.10.refs_3_ = bf16[2,32,128]{2,1,0:T(8,128)(2,1)S(1)} collective-permute-done((bf16[2,32,128]{2,1,0:T(8,128)(2,1)S(1)}, bf16[2,32,128]{2,1,0:T(8,128)(2,1)S(1)}, u32[]{:S(2)}, u32[]{:S(2)}) %collective-permute-start.10) | collective-permute-done | bytes 16416 | tf_op jit(solution)/shard_map/ppermute | solution.py:115
  45.3 1.3 %collective-permute-done.9.refs_2_ = bf16[2,32,128]{2,1,0:T(8,128)(2,1)S(1)} collective-permute-done((bf16[2,32,128]{2,1,0:T(8,128)(2,1)S(1)}, bf16[2,32,128]{2,1,0:T(8,128)(2,1)S(1)}, u32[]{:S(2)}, u32[]{:S(2)}) %collective-permute-start.9) | collective-permute-done | bytes 16416 | tf_op jit(solution)/shard_map/ppermute | solution.py:115
  46.7 0.8 %collective-permute-start.11 = (bf16[4,2,32,128]{3,2,1,0:T(8,128)(2,1)S(1)}, bf16[4,2,32,128]{3,2,1,0:T(8,128)(2,1)S(1)}, u32[]{:S(2)}, u32[]{:S(2)}) collective-permute-start(bf16[4,2,32,128]{3,2,1,0:T(8,128)(2,1)S(1)} %shard_map.185.refs_0_), channel_id=1, source_target_pairs={{0,1},{1,0},{2,3},{3,2},{4,5},{5,4},{6,7},{7,6},{8,9},{9,8},{10,11... | collective-permute-start | bytes 196616 | tf_op jit(solution)/shard_map/ppermute | solution.py:115
  47.4 1.1 %collective-permute-start.12 = (bf16[4,2,32,128]{3,2,1,0:T(8,128)(2,1)S(1)}, bf16[4,2,32,128]{3,2,1,0:T(8,128)(2,1)S(1)}, u32[]{:S(2)}, u32[]{:S(2)}) collective-permute-start(bf16[4,2,32,128]{3,2,1,0:T(8,128)(2,1)S(1)} %shard_map.185.refs_0_), channel_id=1, source_target_pairs={{0,2},{1,3},{2,0},{3,1},{4,6},{5,7},{6,4},{7,5},{8,10},{9,11},{10,... | collective-permute-start | bytes 196616 | tf_op jit(solution)/shard_map/ppermute | solution.py:115
  48.6 2.6 %collective-permute-start.13 = (bf16[4,2,32,128]{3,2,1,0:T(8,128)(2,1)S(1)}, bf16[4,2,32,128]{3,2,1,0:T(8,128)(2,1)S(1)}, u32[]{:S(2)}, u32[]{:S(2)}) collective-permute-start(bf16[4,2,32,128]{3,2,1,0:T(8,128)(2,1)S(1)} %shard_map.185.refs_0_), channel_id=1, source_target_pairs={{0,3},{1,2},{2,1},{3,0},{4,7},{5,6},{6,5},{7,4},{8,11},{9,10},{10,... | collective-permute-start | bytes 196616 | tf_op jit(solution)/shard_map/ppermute | solution.py:115
  51.1 1.0 %shard_map.182 = (bf16[512,128]{1,0:T(8,128)(2,1)}, bf16[512,128]{1,0:T(8,128)(2,1)}) custom-call(f32[1,512]{1,0:T(1,128)S(1)} %get-tuple-element.96.refs_8_.scale, f32[1,128]{1,0:T(1,128)S(1)} %get-tuple-element.72.cross_gain_ref.gain, f32[128,512]{1,0:T(8,128)S(1)} %get-tuple-element.93.refs_2_.attended, ...), custom_call_target="tpu_custom_call" | custom-call | flops 33554432 | bytes 920064 | tf_op jit(solution)/shard_map/pallas_call | solution.py:43
  52.1 1.9 %shard_map.180 = (f32[512,128]{1,0:T(8,128)S(1)}, f32[512,128]{1,0:T(8,128)S(1)}, bf16[512,128]{1,0:T(8,128)(2,1)}, bf16[512,128]{1,0:T(8,128)(2,1)}) custom-call(f32[128,512]{1,0:T(8,128)S(1)} %get-tuple-element.97.grad, f32[1,512]{1,0:T(1,128)S(1)} %get-tuple-element.98.scale, f32[1,512]{1,0:T(1,128)S(1)} %get-tuple-element.99.delta, ...), custom_call_target="tpu_custom_call" | custom-call | flops 335544320 | bytes 2890240 | tf_op jit(solution)/shard_map/pallas_call | solution.py:43
  54.0 0.7 %collective-permute-done.13.refs_3_ = bf16[4,2,32,128]{3,2,1,0:T(8,128)(2,1)S(1)} collective-permute-done((bf16[4,2,32,128]{3,2,1,0:T(8,128)(2,1)S(1)}, bf16[4,2,32,128]{3,2,1,0:T(8,128)(2,1)S(1)}, u32[]{:S(2)}, u32[]{:S(2)}) %collective-permute-start.13) | collective-permute-done | bytes 65568 | tf_op jit(solution)/shard_map/ppermute | solution.py:115
  54.7 0.8 %shard_map.186 = (bf16[32,2048]{1,0:T(8,128)(2,1)}, bf16[32,2048]{1,0:T(8,128)(2,1)}) custom-call(bf16[4,2,32,128]{3,2,1,0:T(8,128)(2,1)S(1)} %shard_map.185.refs_0_, bf16[4,2,32,128]{3,2,1,0:T(8,128)(2,1)S(1)} %collective-permute-done.11.refs_1_, bf16[4,2,32,128]{3,2,1,0:T(8,128)(2,1)S(1)} %collective-permute-done.12.refs_2_, ...), custom_call_target="tpu_custom_call" | custom-call | bytes 524288 | tf_op jit(solution)/shard_map/pallas_call | solution.py:43
  55.5 0.7 %shard_map.183 = (bf16[512,128]{1,0:T(8,128)(2,1)}, bf16[512,128]{1,0:T(8,128)(2,1)}) custom-call(f32[512,128]{1,0:T(8,128)S(1)} %get-tuple-element.110.own_key_ref, f32[512,128]{1,0:T(8,128)S(1)} %get-tuple-element.111.own_value_ref, bf16[2,512,128]{2,1,0:T(8,128)(2,1)S(1)} %collective-permute-done.6.refs_0_), custom_call_target="tpu_custom_call" | custom-call | bytes 1048576 | tf_op jit(solution)/shard_map/pallas_call | solution.py:43
  (22 shorter events, 3.1 us)
Async XLA Ops:
  0.6 16.8 %collective-permute-start = (bf16[512,128]{1,0:T(8,128)(2,1)}, bf16[512,128]{1,0:T(8,128)(2,1)S(1)}, u32[]{:S(2)}, u32[]{:S(2)}) collective-permute-start(bf16[512,128]{1,0:T(8,128)(2,1)} %refs_1_.1), channel_id=1, source_target_pairs={{0,4},{4,0},{1,5},{5,1},{2,6},{6,2},{3,7},{7,3},{8,12},{12,8},{9,1... | collective-permute-start | bytes 393224 | tf_op jit(solution)/shard_map/ppermute | solution.py:105
  3.7 14.4 %collective-permute-start.5 = (bf16[512,128]{1,0:T(8,128)(2,1)}, bf16[512,128]{1,0:T(8,128)(2,1)S(1)}, u32[]{:S(2)}, u32[]{:S(2)}) collective-permute-start(bf16[512,128]{1,0:T(8,128)(2,1)} %refs_2_.1), channel_id=1, source_target_pairs={{0,4},{4,0},{1,5},{5,1},{2,6},{6,2},{3,7},{7,3},{8,12},{12,8},{9,1... | collective-permute-start | bytes 393224 | tf_op jit(solution)/shard_map/ppermute | solution.py:105
  4.6 7.0 %collective-permute-start.1 = (bf16[4,2,32,128]{3,2,1,0:T(8,128)(2,1)S(1)}, bf16[4,2,32,128]{3,2,1,0:T(8,128)(2,1)S(1)}, u32[]{:S(2)}, u32[]{:S(2)}) collective-permute-start(bf16[4,2,32,128]{3,2,1,0:T(8,128)(2,1)S(1)} %shard_map.173.refs_0_), channel_id=1, source_target_pairs={{0,4},{4,0},{1,5},{5,1},{2,6},{6,2},{3,7},{7,3},{8,12},{12,8},{9,1... | collective-permute-start | bytes 196616 | tf_op jit(solution)/shard_map/ppermute | solution.py:105
  11.6 4.0 %collective-permute-start.2 = (bf16[2,2,32,128]{3,2,1,0:T(8,128)(2,1)S(1)}, bf16[2,2,32,128]{3,2,1,0:T(8,128)(2,1)S(1)}, u32[]{:S(2)}, u32[]{:S(2)}) collective-permute-start(bf16[2,2,32,128]{3,2,1,0:T(8,128)(2,1)S(1)} %get-tuple-element.83), channel_id=1, source_target_pairs={{0,8},{8,0},{16,24},{24,16},{1,9},{9,1},{17,25},{25,17},{2,10},{10... | collective-permute-start | bytes 98312 | tf_op jit(solution)/shard_map/ppermute | solution.py:115
  11.7 4.0 %collective-permute-start.3 = (bf16[2,2,32,128]{3,2,1,0:T(8,128)(2,1)S(1)}, bf16[2,2,32,128]{3,2,1,0:T(8,128)(2,1)S(1)}, u32[]{:S(2)}, u32[]{:S(2)}) collective-permute-start(bf16[2,2,32,128]{3,2,1,0:T(8,128)(2,1)S(1)} %get-tuple-element.84), channel_id=1, source_target_pairs={{0,16},{8,24},{16,0},{24,8},{1,17},{9,25},{17,1},{25,9},{2,18},{10... | collective-permute-start | bytes 98312 | tf_op jit(solution)/shard_map/ppermute | solution.py:115
  13.5 3.4 %collective-permute-start.4 = (bf16[2,2,32,128]{3,2,1,0:T(8,128)(2,1)S(1)}, bf16[2,2,32,128]{3,2,1,0:T(8,128)(2,1)S(1)}, u32[]{:S(2)}, u32[]{:S(2)}) collective-permute-start(bf16[2,2,32,128]{3,2,1,0:T(8,128)(2,1)S(1)} %get-tuple-element.85), channel_id=1, source_target_pairs={{0,24},{8,16},{16,8},{24,0},{1,25},{9,17},{17,9},{25,1},{2,26},{10... | collective-permute-start | bytes 98312 | tf_op jit(solution)/shard_map/ppermute | solution.py:115
  32.3 23.2 %collective-permute-start.6 = (bf16[2,512,128]{2,1,0:T(8,128)(2,1)S(1)}, bf16[2,512,128]{2,1,0:T(8,128)(2,1)S(1)}, u32[]{:S(2)}, u32[]{:S(2)}) collective-permute-start(bf16[2,512,128]{2,1,0:T(8,128)(2,1)S(1)} %get-tuple-element.112), channel_id=1, source_target_pairs={{0,4},{4,0},{1,5},{5,1},{2,6},{6,2},{3,7},{7,3},{8,12},{12,8},{9,1... | collective-permute-start | bytes 786440 | tf_op jit(solution)/shard_map/ppermute | solution.py:105
  33.8 8.2 %collective-permute-start.7 = (bf16[2,128,128]{2,1,0:T(8,128)(2,1)S(1)}, bf16[2,128,128]{2,1,0:T(8,128)(2,1)S(1)}, u32[]{:S(2)}, u32[]{:S(2)}) collective-permute-start(bf16[2,128,128]{2,1,0:T(8,128)(2,1)S(1)} %get-tuple-element.117), channel_id=1, source_target_pairs={{0,4},{4,0},{1,5},{5,1},{2,6},{6,2},{3,7},{7,3},{8,12},{12,8},{9,1... | collective-permute-start | bytes 196616 | tf_op jit(solution)/shard_map/ppermute | solution.py:105
  42.1 3.2 %collective-permute-start.10 = (bf16[2,32,128]{2,1,0:T(8,128)(2,1)S(1)}, bf16[2,32,128]{2,1,0:T(8,128)(2,1)S(1)}, u32[]{:S(2)}, u32[]{:S(2)}) collective-permute-start(bf16[2,32,128]{2,1,0:T(8,128)(2,1)S(1)} %get-tuple-element.121), channel_id=1, source_target_pairs={{0,24},{8,16},{16,8},{24,0},{1,25},{9,17},{17,9},{25,1},{2,26},{10... | collective-permute-start | bytes 49160 | tf_op jit(solution)/shard_map/ppermute | solution.py:115
  42.2 3.2 %collective-permute-start.8 = (bf16[2,32,128]{2,1,0:T(8,128)(2,1)S(1)}, bf16[2,32,128]{2,1,0:T(8,128)(2,1)S(1)}, u32[]{:S(2)}, u32[]{:S(2)}) collective-permute-start(bf16[2,32,128]{2,1,0:T(8,128)(2,1)S(1)} %get-tuple-element.119), channel_id=1, source_target_pairs={{0,8},{8,0},{16,24},{24,16},{1,9},{9,1},{17,25},{25,17},{2,10},{10... | collective-permute-start | bytes 49160 | tf_op jit(solution)/shard_map/ppermute | solution.py:115
  42.9 3.7 %collective-permute-start.9 = (bf16[2,32,128]{2,1,0:T(8,128)(2,1)S(1)}, bf16[2,32,128]{2,1,0:T(8,128)(2,1)S(1)}, u32[]{:S(2)}, u32[]{:S(2)}) collective-permute-start(bf16[2,32,128]{2,1,0:T(8,128)(2,1)S(1)} %get-tuple-element.120), channel_id=1, source_target_pairs={{0,16},{8,24},{16,0},{24,8},{1,17},{9,25},{17,1},{25,9},{2,18},{10... | collective-permute-start | bytes 49160 | tf_op jit(solution)/shard_map/ppermute | solution.py:115
  46.7 7.4 %collective-permute-start.11 = (bf16[4,2,32,128]{3,2,1,0:T(8,128)(2,1)S(1)}, bf16[4,2,32,128]{3,2,1,0:T(8,128)(2,1)S(1)}, u32[]{:S(2)}, u32[]{:S(2)}) collective-permute-start(bf16[4,2,32,128]{3,2,1,0:T(8,128)(2,1)S(1)} %shard_map.185.refs_0_), channel_id=1, source_target_pairs={{0,1},{1,0},{2,3},{3,2},{4,5},{5,4},{6,7},{7,6},{8,9},{9,8},{10,11... | collective-permute-start | bytes 196616 | tf_op jit(solution)/shard_map/ppermute | solution.py:115
  47.4 6.6 %collective-permute-start.12 = (bf16[4,2,32,128]{3,2,1,0:T(8,128)(2,1)S(1)}, bf16[4,2,32,128]{3,2,1,0:T(8,128)(2,1)S(1)}, u32[]{:S(2)}, u32[]{:S(2)}) collective-permute-start(bf16[4,2,32,128]{3,2,1,0:T(8,128)(2,1)S(1)} %shard_map.185.refs_0_), channel_id=1, source_target_pairs={{0,2},{1,3},{2,0},{3,1},{4,6},{5,7},{6,4},{7,5},{8,10},{9,11},{10,... | collective-permute-start | bytes 196616 | tf_op jit(solution)/shard_map/ppermute | solution.py:115
  48.6 6.2 %collective-permute-start.13 = (bf16[4,2,32,128]{3,2,1,0:T(8,128)(2,1)S(1)}, bf16[4,2,32,128]{3,2,1,0:T(8,128)(2,1)S(1)}, u32[]{:S(2)}, u32[]{:S(2)}) collective-permute-start(bf16[4,2,32,128]{3,2,1,0:T(8,128)(2,1)S(1)} %shard_map.185.refs_0_), channel_id=1, source_target_pairs={{0,3},{1,2},{2,1},{3,0},{4,7},{5,6},{6,5},{7,4},{8,11},{9,10},{10,... | collective-permute-start | bytes 196616 | tf_op jit(solution)/shard_map/ppermute | solution.py:115

commit v2 on v1

--- a/solution.py
+++ b/solution.py
@@ -369,12 +369,12 @@
             halves = [entry[:, at : at + half] for entry in lines for at in (0, half)]
             tile = jnp.concatenate(halves, axis=0)
             for at in range(peers):
-                packed[at] = tile
+                packed[at] = tile.astype(BF16)
 
         self_attended, self_stats, packed = call(
             other_values_seen,
             [first_weighted, first_weight, other_weight, self_lifted, cross_stats] + other_values + other_stores,
-            [(tall, F32), ((2, frames), F32), ((peers, 8, half), F32)],
+            [(tall, F32), ((2, frames), F32), ((peers, 8, half), BF16)],
             flops=frames * unit * others,
         )
 
@@ -382,9 +382,9 @@
         received = [lax.all_to_all(packed, ("sec", "tp"), split_axis=0, concat_axis=0, tiled=True)]
 
         def norm_terms(received_ref, stats, attended, lifted, at):
-            sums = received_ref[0][0]
+            sums = received_ref[0][0].astype(F32)
             for source in range(1, peers):
-                sums = sums + received_ref[0][source]
+                sums = sums + received_ref[0][source].astype(F32)
             joined = [
                 jnp.concatenate([sums[2 * pick : 2 * pick + 1], sums[2 * pick + 1 : 2 * pick + 2]], axis=1)
                 for pick in (2 * at, 2 * at + 1)
@@ -396,7 +396,7 @@
             delta = scale * (stats[1:2, :] - curve * stats[0:1, :])
             return scale, delta, grad
 
-        def block_grads(key_grad, value_grad, value, store, weight, delta, grad_tall, grad_wide, query, slopes):
+        def block_grads(key_grad, value_grad, value, store, weight, delta, grad_tall, grad_folded, query, slopes):
             count, step = value.shape[0], 128
             step = min(step, count)
             for at in range(0, count, step):
@@ -405,10 +405,10 @@
                 slope = (probs.astype(F32) * ((products - delta) * weight)).astype(BF16)
                 slopes[at : at + step, :] = slope
                 key_grad(at, step, dot_nn(slope, query) * scaling)
-                value_grad(at, step, dot_nn(probs, grad_wide))
+                value_grad(at, step, dot_nt(probs, grad_folded))
 
         def memory_grads(block, store, factor, delta, grad, query, out, slopes):
-            grad_wide = (grad * factor).T.astype(BF16)
+            grad_folded = (grad * factor).astype(BF16)
 
             def key_grad(first, count, value):
                 out[0, first : first + count, :] = value.astype(out.dtype)
@@ -424,7 +424,7 @@
                 factor,
                 delta,
                 grad.astype(BF16),
-                grad_wide,
+                grad_folded,
                 query[...],
                 slopes,
             )
@@ -515,7 +515,7 @@
             grad_tall = grad.astype(BF16)
             for by in range(others):
                 line_weight = weight[by : by + 1, :]
-                grad_wide = (grad * line_weight).T.astype(BF16)
+                grad_folded = (grad * line_weight).astype(BF16)
 
                 def key_grad(first, count, value, out=pairs_out[by]):
                     out[0, first : first + count, :] = value.astype(BF16)
@@ -531,7 +531,7 @@
                     line_weight,
                     delta,
                     grad_tall,
-                    grad_wide,
+                    grad_folded,
                     query[...],
                     slopes[by],
                 )
@@ -557,7 +557,7 @@
             key_out, value_out, query_out, out, own_slopes = refs[2 * others :]
             grad_tall = grad[...].astype(BF16)
             line_weight = weight[...]
-            grad_wide = (grad[...] * line_weight).T.astype(BF16)
+            grad_folded = (grad[...] * line_weight).astype(BF16)
 
             def key_grad(first, count, result):
                 key_out[first : first + count, :] = result
@@ -573,7 +573,7 @@
                 line_weight,
                 delta[...],
                 grad_tall,
-                grad_wide,
+                grad_folded,
                 query[...],
                 own_slopes,
             )

time: 56.4 us -> 55.4 us (0.982)
  blocking collectives: 12.4 us -> 11.7 us
    all_to_all x1, blocking collectives: 12.4 us -> 11.7 us  [per_device(): lax.all_to_all(packed, ('sec', 'tp'), split_axis=0, concat_axis=0, tiled=...]
  transfers between devices with their start and end apart: 14 -> 14, of which waited for: 6 -> 5; matrix products, arithmetic and copies ran while one was open for 0% -> 0% of each run, Pallas kernels for 14% -> 15%
where the time goes in v2:
time: 55.4 us; the launch traced here: 55.2 us
  waiting for transfers between devices  16.7 us (30%)
  starting transfers between devices  15.5 us (28%)
  blocking collectives  11.7 us (21%)
  Pallas kernels  10.5 us (19%)
  between operations  0.75 us (1%)
    ppermute x5, waiting for transfers between devices, shifted(): lax.ppermute(value, axis, [(at, (at + by) % count) for at in range(count)])  12.3 us
    all_to_all x1, blocking collectives, per_device(): lax.all_to_all(packed, ('sec', 'tp'), split_axis=0, concat_axis=0, tiled=...  11.7 us
    pallas_call x17, Pallas kernels, call(): pl.pallas_call(body, out_shape=shapes, in_specs=[SMEM] * smem + [space] *...  10.5 us
    ppermute x9, starting transfers between devices, swapped(): return lax.ppermute(value, axis, [(at, at ^ by) for at in range(count)])  8.31 us
    ppermute x5, starting transfers between devices, shifted(): lax.ppermute(value, axis, [(at, (at + by) % count) for at in range(count)])  7.21 us
    ppermute x9, waiting for transfers between devices, swapped(): return lax.ppermute(value, axis, [(at, at ^ by) for at in range(count)])  4.36 us
  transfers between devices with their start and end apart: 14, of which 5 were waited for; matrix products, arithmetic and copies ran while one was open for 0% of the time, Pallas kernels for 15%

profile of v2, /device:TPU:0, one launch (start us, length us, event | category | flops | bytes accessed | tf_op | source)
XLA Modules:
  0.0 55.2 jit_solution(2281102262430183737)
XLA Ops:
  0.6 3.0 %collective-permute-start = (bf16[512,128]{1,0:T(8,128)(2,1)}, bf16[512,128]{1,0:T(8,128)(2,1)S(1)}, u32[]{:S(2)}, u32[]{:S(2)}) collective-permute-start(bf16[512,128]{1,0:T(8,128)(2,1)} %refs_1_.1), channel_id=1, source_target_pairs={{0,4},{4,0},{1,5},{5,1},{2,6},{6,2},{3,7},{7,3},{8,12},{12,8},{9,1... | collective-permute-start | bytes 393224 | tf_op jit(solution)/shard_map/ppermute | solution.py:105
  3.7 0.9 %shard_map.173.refs_0_ = bf16[4,2,32,128]{3,2,1,0:T(8,128)(2,1)S(1)} custom-call(bf16[32,2048]{1,0:T(8,128)(2,1)} %key_ref.1, bf16[32,2048]{1,0:T(8,128)(2,1)} %value_ref.1), custom_call_target="tpu_custom_call" | custom-call | bytes 327680 | tf_op jit(solution)/shard_map/pallas_call | solution.py:43
  4.6 2.0 %collective-permute-start.1 = (bf16[4,2,32,128]{3,2,1,0:T(8,128)(2,1)S(1)}, bf16[4,2,32,128]{3,2,1,0:T(8,128)(2,1)S(1)}, u32[]{:S(2)}, u32[]{:S(2)}) collective-permute-start(bf16[4,2,32,128]{3,2,1,0:T(8,128)(2,1)S(1)} %shard_map.173.refs_0_), channel_id=1, source_target_pairs={{0,4},{4,0},{1,5},{5,1},{2,6},{6,2},{3,7},{7,3},{8,12},{12,8},{9,1... | collective-permute-start | bytes 196616 | tf_op jit(solution)/shard_map/ppermute | solution.py:105
  6.6 4.9 %collective-permute-done.1.refs_1_ = bf16[4,2,32,128]{3,2,1,0:T(8,128)(2,1)S(1)} collective-permute-done((bf16[4,2,32,128]{3,2,1,0:T(8,128)(2,1)S(1)}, bf16[4,2,32,128]{3,2,1,0:T(8,128)(2,1)S(1)}, u32[]{:S(2)}, u32[]{:S(2)}) %collective-permute-start.1) | collective-permute-done | bytes 65568 | tf_op jit(solution)/shard_map/ppermute | solution.py:105
  11.7 1.8 %collective-permute-start.3 = (bf16[2,2,32,128]{3,2,1,0:T(8,128)(2,1)S(1)}, bf16[2,2,32,128]{3,2,1,0:T(8,128)(2,1)S(1)}, u32[]{:S(2)}, u32[]{:S(2)}) collective-permute-start(bf16[2,2,32,128]{3,2,1,0:T(8,128)(2,1)S(1)} %get-tuple-element.84), channel_id=1, source_target_pairs={{0,16},{8,24},{16,0},{24,8},{1,17},{9,25},{17,1},{25,9},{2,18},{10... | collective-permute-start | bytes 98312 | tf_op jit(solution)/shard_map/ppermute | solution.py:115
  13.6 1.3 %shard_map.170 = (bf16[512,128]{1,0:T(8,128)(2,1)S(1)}, bf16[512,128]{1,0:T(8,128)(2,1)S(1)}, bf16[512,128]{1,0:T(8,128)(2,1)S(1)}, bf16[512,128]{1,0:T(8,128)(2...) custom-call(s32[8]{0:T(128)} %start_ref.1, ...), custom_call_target="tpu_custom_call" | custom-call | bytes 1591328 | tf_op jit(solution)/shard_map/pallas_call | solution.py:43
  14.8 0.8 %shard_map.171 = (bf16[512,512]{1,0:T(8,128)(2,1)S(1)}, f32[1,512]{1,0:T(1,128)S(1)}, f32[1,512]{1,0:T(1,128)S(1)}, f32[128,512]{1,0:T(8,128)S(1)}, f32[128,512]{1,0:T(8,128)S(1)}, /*index=5*/f32[128,512]{1,0:T(8,128)S(1)}) custom-call(s32[8,512]{1,0:T(8,128)S(1)} %get-tuple-element.66.base, bf16[512,128]{1,0:T(8,128)(2,1)S(1)} %get-tuple-element.67.query.refs_5_, ...), custom_call_target="tpu_custom_call" | custom-call | flops 134217728 | bytes 1987584 | tf_op jit(solution)/shard_map/pallas_call | solution.py:43
  15.7 1.2 %collective-permute-done.4.refs_3_ = bf16[2,2,32,128]{3,2,1,0:T(8,128)(2,1)S(1)} collective-permute-done((bf16[2,2,32,128]{3,2,1,0:T(8,128)(2,1)S(1)}, bf16[2,2,32,128]{3,2,1,0:T(8,128)(2,1)S(1)}, u32[]{:S(2)}, u32[]{:S(2)}) %collective-permute-start.4) | collective-permute-done | bytes 32800 | tf_op jit(solution)/shard_map/ppermute | solution.py:115
  16.9 0.6 %shard_map.176 = (bf16[128,512]{1,0:T(8,128)(2,1)S(1)}, bf16[128,512]{1,0:T(8,128)(2,1)S(1)}, f32[2,512]{1,0:T(2,128)S(1)}, f32[128,512]{1,0:T(8,128)S(1)}, f32[2,512]{1,0:T(2,128)S(1)}) custom-call(bf16[512,128]{1,0:T(8,128)(2,1)S(1)} %get-tuple-element.80.query.refs_5_, f32[128,512]{1,0:T(8,128)S(1)} %get-tuple-element.81.lifted.refs_3_, ...), custom_call_target="tpu_custom_call" | custom-call | flops 67108864 | bytes 1056768 | tf_op jit(solution)/shard_map/pallas_call | solution.py:43
  18.3 11.7 %all_to_all.5.refs_0_ = bf16[16,8,256]{2,1,0:T(8,128)(2,1)S(1)} all-to-all(bf16[16,8,256]{2,1,0:T(8,128)(2,1)S(1)} %get-tuple-element.90), channel_id=1, replica_groups=mesh['sec'=4,'ctx'=2,'tp'=4] {'sec','tp'}, dimensions={0} | all-to-all | bytes 131072 | tf_op jit(solution)/shard_map/all_to_all | solution.py:382
  30.4 1.0 %shard_map.179 = (bf16[2,512,128]{2,1,0:T(8,128)(2,1)S(1)}, bf16[512,512]{1,0:T(8,128)(2,1)S(1)}, f32[128,512]{1,0:T(8,128)S(1)}, f32[1,512]{1,0:T(1,128)S(1)}, f32[1,512]{1,0:T(1,128)S(1)}) custom-call(bf16[16,8,256]{2,1,0:T(8,128)(2,1)S(1)} %all_to_all.5.refs_0_, f32[2,512]{1,0:T(2,128)S(1)} %get-tuple-element.91.refs_1_, ...), custom_call_target="tpu_custom_call" | custom-call | flops 201326592 | bytes 2435072 | tf_op jit(solution)/shard_map/pallas_call | solution.py:43
  31.4 1.5 %collective-permute-start.6 = (bf16[2,512,128]{2,1,0:T(8,128)(2,1)S(1)}, bf16[2,512,128]{2,1,0:T(8,128)(2,1)S(1)}, u32[]{:S(2)}, u32[]{:S(2)}) collective-permute-start(bf16[2,512,128]{2,1,0:T(8,128)(2,1)S(1)} %get-tuple-element.112), channel_id=1, source_target_pairs={{0,4},{4,0},{1,5},{5,1},{2,6},{6,2},{3,7},{7,3},{8,12},{12,8},{9,1... | collective-permute-start | bytes 786440 | tf_op jit(solution)/shard_map/ppermute | solution.py:105
  33.9 7.3 %collective-permute-done.7.refs_1_ = bf16[2,128,128]{2,1,0:T(8,128)(2,1)S(1)} collective-permute-done((bf16[2,128,128]{2,1,0:T(8,128)(2,1)S(1)}, bf16[2,128,128]{2,1,0:T(8,128)(2,1)S(1)}, u32[]{:S(2)}, u32[]{:S(2)}) %collective-permute-start.7) | collective-permute-done | bytes 65568 | tf_op jit(solution)/shard_map/ppermute | solution.py:105
  41.3 0.6 %collective-permute-start.9 = (bf16[2,32,128]{2,1,0:T(8,128)(2,1)S(1)}, bf16[2,32,128]{2,1,0:T(8,128)(2,1)S(1)}, u32[]{:S(2)}, u32[]{:S(2)}) collective-permute-start(bf16[2,32,128]{2,1,0:T(8,128)(2,1)S(1)} %get-tuple-element.120), channel_id=1, source_target_pairs={{0,16},{8,24},{16,0},{24,8},{1,17},{9,25},{17,1},{25,9},{2,18},{10... | collective-permute-start | bytes 49160 | tf_op jit(solution)/shard_map/ppermute | solution.py:115
  42.0 1.2 %collective-permute-start.10 = (bf16[2,32,128]{2,1,0:T(8,128)(2,1)S(1)}, bf16[2,32,128]{2,1,0:T(8,128)(2,1)S(1)}, u32[]{:S(2)}, u32[]{:S(2)}) collective-permute-start(bf16[2,32,128]{2,1,0:T(8,128)(2,1)S(1)} %get-tuple-element.121), channel_id=1, source_target_pairs={{0,24},{8,16},{16,8},{24,0},{1,25},{9,17},{17,9},{25,1},{2,26},{10... | collective-permute-start | bytes 49160 | tf_op jit(solution)/shard_map/ppermute | solution.py:115
  43.2 2.1 %collective-permute-done.9.refs_2_ = bf16[2,32,128]{2,1,0:T(8,128)(2,1)S(1)} collective-permute-done((bf16[2,32,128]{2,1,0:T(8,128)(2,1)S(1)}, bf16[2,32,128]{2,1,0:T(8,128)(2,1)S(1)}, u32[]{:S(2)}, u32[]{:S(2)}) %collective-permute-start.9) | collective-permute-done | bytes 16416 | tf_op jit(solution)/shard_map/ppermute | solution.py:115
  45.3 0.8 %collective-permute-start.13 = (bf16[4,2,32,128]{3,2,1,0:T(8,128)(2,1)S(1)}, bf16[4,2,32,128]{3,2,1,0:T(8,128)(2,1)S(1)}, u32[]{:S(2)}, u32[]{:S(2)}) collective-permute-start(bf16[4,2,32,128]{3,2,1,0:T(8,128)(2,1)S(1)} %shard_map.185.refs_0_), channel_id=1, source_target_pairs={{0,3},{1,2},{2,1},{3,0},{4,7},{5,6},{6,5},{7,4},{8,11},{9,10},{10,... | collective-permute-start | bytes 196616 | tf_op jit(solution)/shard_map/ppermute | solution.py:115
  46.1 1.1 %collective-permute-start.12 = (bf16[4,2,32,128]{3,2,1,0:T(8,128)(2,1)S(1)}, bf16[4,2,32,128]{3,2,1,0:T(8,128)(2,1)S(1)}, u32[]{:S(2)}, u32[]{:S(2)}) collective-permute-start(bf16[4,2,32,128]{3,2,1,0:T(8,128)(2,1)S(1)} %shard_map.185.refs_0_), channel_id=1, source_target_pairs={{0,2},{1,3},{2,0},{3,1},{4,6},{5,7},{6,4},{7,5},{8,10},{9,11},{10,... | collective-permute-start | bytes 196616 | tf_op jit(solution)/shard_map/ppermute | solution.py:115
  47.2 2.6 %collective-permute-start.11 = (bf16[4,2,32,128]{3,2,1,0:T(8,128)(2,1)S(1)}, bf16[4,2,32,128]{3,2,1,0:T(8,128)(2,1)S(1)}, u32[]{:S(2)}, u32[]{:S(2)}) collective-permute-start(bf16[4,2,32,128]{3,2,1,0:T(8,128)(2,1)S(1)} %shard_map.185.refs_0_), channel_id=1, source_target_pairs={{0,1},{1,0},{2,3},{3,2},{4,5},{5,4},{6,7},{7,6},{8,9},{9,8},{10,11... | collective-permute-start | bytes 196616 | tf_op jit(solution)/shard_map/ppermute | solution.py:115
  49.8 1.0 %shard_map.182 = (bf16[512,128]{1,0:T(8,128)(2,1)}, bf16[512,128]{1,0:T(8,128)(2,1)}) custom-call(f32[1,512]{1,0:T(1,128)S(1)} %get-tuple-element.96.refs_8_.scale, f32[1,128]{1,0:T(1,128)S(1)} %get-tuple-element.72.cross_gain_ref.gain, f32[128,512]{1,0:T(8,128)S(1)} %get-tuple-element.93.refs_2_.attended, ...), custom_call_target="tpu_custom_call" | custom-call | flops 33554432 | bytes 920064 | tf_op jit(solution)/shard_map/pallas_call | solution.py:43
  50.8 1.9 %shard_map.180 = (f32[512,128]{1,0:T(8,128)S(1)}, f32[512,128]{1,0:T(8,128)S(1)}, bf16[512,128]{1,0:T(8,128)(2,1)}, bf16[512,128]{1,0:T(8,128)(2,1)}) custom-call(f32[128,512]{1,0:T(8,128)S(1)} %get-tuple-element.97.grad, f32[1,512]{1,0:T(1,128)S(1)} %get-tuple-element.98.scale, f32[1,512]{1,0:T(1,128)S(1)} %get-tuple-element.99.delta, ...), custom_call_target="tpu_custom_call" | custom-call | flops 335544320 | bytes 2890240 | tf_op jit(solution)/shard_map/pallas_call | solution.py:43
  52.7 1.0 %collective-permute-done.12.refs_2_ = bf16[4,2,32,128]{3,2,1,0:T(8,128)(2,1)S(1)} collective-permute-done((bf16[4,2,32,128]{3,2,1,0:T(8,128)(2,1)S(1)}, bf16[4,2,32,128]{3,2,1,0:T(8,128)(2,1)S(1)}, u32[]{:S(2)}, u32[]{:S(2)}) %collective-permute-start.12) | collective-permute-done | bytes 65568 | tf_op jit(solution)/shard_map/ppermute | solution.py:115
  53.7 0.8 %shard_map.186 = (bf16[32,2048]{1,0:T(8,128)(2,1)}, bf16[32,2048]{1,0:T(8,128)(2,1)}) custom-call(bf16[4,2,32,128]{3,2,1,0:T(8,128)(2,1)S(1)} %shard_map.185.refs_0_, bf16[4,2,32,128]{3,2,1,0:T(8,128)(2,1)S(1)} %collective-permute-done.11.refs_1_, bf16[4,2,32,128]{3,2,1,0:T(8,128)(2,1)S(1)} %collective-permute-done.12.refs_2_, ...), custom_call_target="tpu_custom_call" | custom-call | bytes 524288 | tf_op jit(solution)/shard_map/pallas_call | solution.py:43
  54.4 0.7 %shard_map.183 = (bf16[512,128]{1,0:T(8,128)(2,1)}, bf16[512,128]{1,0:T(8,128)(2,1)}) custom-call(f32[512,128]{1,0:T(8,128)S(1)} %get-tuple-element.110.own_key_ref, f32[512,128]{1,0:T(8,128)S(1)} %get-tuple-element.111.own_value_ref, bf16[2,512,128]{2,1,0:T(8,128)(2,1)S(1)} %collective-permute-done.6.refs_0_), custom_call_target="tpu_custom_call" | custom-call | bytes 1048576 | tf_op jit(solution)/shard_map/pallas_call | solution.py:43
  (22 shorter events, 2.5 us)
Async XLA Ops:
  0.6 16.8 %collective-permute-start = (bf16[512,128]{1,0:T(8,128)(2,1)}, bf16[512,128]{1,0:T(8,128)(2,1)S(1)}, u32[]{:S(2)}, u32[]{:S(2)}) collective-permute-start(bf16[512,128]{1,0:T(8,128)(2,1)} %refs_1_.1), channel_id=1, source_target_pairs={{0,4},{4,0},{1,5},{5,1},{2,6},{6,2},{3,7},{7,3},{8,12},{12,8},{9,1... | collective-permute-start | bytes 393224 | tf_op jit(solution)/shard_map/ppermute | solution.py:105
  3.7 14.4 %collective-permute-start.5 = (bf16[512,128]{1,0:T(8,128)(2,1)}, bf16[512,128]{1,0:T(8,128)(2,1)S(1)}, u32[]{:S(2)}, u32[]{:S(2)}) collective-permute-start(bf16[512,128]{1,0:T(8,128)(2,1)} %refs_2_.1), channel_id=1, source_target_pairs={{0,4},{4,0},{1,5},{5,1},{2,6},{6,2},{3,7},{7,3},{8,12},{12,8},{9,1... | collective-permute-start | bytes 393224 | tf_op jit(solution)/shard_map/ppermute | solution.py:105
  4.6 7.0 %collective-permute-start.1 = (bf16[4,2,32,128]{3,2,1,0:T(8,128)(2,1)S(1)}, bf16[4,2,32,128]{3,2,1,0:T(8,128)(2,1)S(1)}, u32[]{:S(2)}, u32[]{:S(2)}) collective-permute-start(bf16[4,2,32,128]{3,2,1,0:T(8,128)(2,1)S(1)} %shard_map.173.refs_0_), channel_id=1, source_target_pairs={{0,4},{4,0},{1,5},{5,1},{2,6},{6,2},{3,7},{7,3},{8,12},{12,8},{9,1... | collective-permute-start | bytes 196616 | tf_op jit(solution)/shard_map/ppermute | solution.py:105
  11.6 4.0 %collective-permute-start.2 = (bf16[2,2,32,128]{3,2,1,0:T(8,128)(2,1)S(1)}, bf16[2,2,32,128]{3,2,1,0:T(8,128)(2,1)S(1)}, u32[]{:S(2)}, u32[]{:S(2)}) collective-permute-start(bf16[2,2,32,128]{3,2,1,0:T(8,128)(2,1)S(1)} %get-tuple-element.83), channel_id=1, source_target_pairs={{0,8},{8,0},{16,24},{24,16},{1,9},{9,1},{17,25},{25,17},{2,10},{10... | collective-permute-start | bytes 98312 | tf_op jit(solution)/shard_map/ppermute | solution.py:115
  11.7 4.0 %collective-permute-start.3 = (bf16[2,2,32,128]{3,2,1,0:T(8,128)(2,1)S(1)}, bf16[2,2,32,128]{3,2,1,0:T(8,128)(2,1)S(1)}, u32[]{:S(2)}, u32[]{:S(2)}) collective-permute-start(bf16[2,2,32,128]{3,2,1,0:T(8,128)(2,1)S(1)} %get-tuple-element.84), channel_id=1, source_target_pairs={{0,16},{8,24},{16,0},{24,8},{1,17},{9,25},{17,1},{25,9},{2,18},{10... | collective-permute-start | bytes 98312 | tf_op jit(solution)/shard_map/ppermute | solution.py:115
  13.5 3.4 %collective-permute-start.4 = (bf16[2,2,32,128]{3,2,1,0:T(8,128)(2,1)S(1)}, bf16[2,2,32,128]{3,2,1,0:T(8,128)(2,1)S(1)}, u32[]{:S(2)}, u32[]{:S(2)}) collective-permute-start(bf16[2,2,32,128]{3,2,1,0:T(8,128)(2,1)S(1)} %get-tuple-element.85), channel_id=1, source_target_pairs={{0,24},{8,16},{16,8},{24,0},{1,25},{9,17},{17,9},{25,1},{2,26},{10... | collective-permute-start | bytes 98312 | tf_op jit(solution)/shard_map/ppermute | solution.py:115
  31.4 23.0 %collective-permute-start.6 = (bf16[2,512,128]{2,1,0:T(8,128)(2,1)S(1)}, bf16[2,512,128]{2,1,0:T(8,128)(2,1)S(1)}, u32[]{:S(2)}, u32[]{:S(2)}) collective-permute-start(bf16[2,512,128]{2,1,0:T(8,128)(2,1)S(1)} %get-tuple-element.112), channel_id=1, source_target_pairs={{0,4},{4,0},{1,5},{5,1},{2,6},{6,2},{3,7},{7,3},{8,12},{12,8},{9,1... | collective-permute-start | bytes 786440 | tf_op jit(solution)/shard_map/ppermute | solution.py:105
  33.0 8.2 %collective-permute-start.7 = (bf16[2,128,128]{2,1,0:T(8,128)(2,1)S(1)}, bf16[2,128,128]{2,1,0:T(8,128)(2,1)S(1)}, u32[]{:S(2)}, u32[]{:S(2)}) collective-permute-start(bf16[2,128,128]{2,1,0:T(8,128)(2,1)S(1)} %get-tuple-element.117), channel_id=1, source_target_pairs={{0,4},{4,0},{1,5},{5,1},{2,6},{6,2},{3,7},{7,3},{8,12},{12,8},{9,1... | collective-permute-start | bytes 196616 | tf_op jit(solution)/shard_map/ppermute | solution.py:105
  41.3 1.9 %collective-permute-start.8 = (bf16[2,32,128]{2,1,0:T(8,128)(2,1)S(1)}, bf16[2,32,128]{2,1,0:T(8,128)(2,1)S(1)}, u32[]{:S(2)}, u32[]{:S(2)}) collective-permute-start(bf16[2,32,128]{2,1,0:T(8,128)(2,1)S(1)} %get-tuple-element.119), channel_id=1, source_target_pairs={{0,8},{8,0},{16,24},{24,16},{1,9},{9,1},{17,25},{25,17},{2,10},{10... | collective-permute-start | bytes 49160 | tf_op jit(solution)/shard_map/ppermute | solution.py:115
  41.3 4.0 %collective-permute-start.9 = (bf16[2,32,128]{2,1,0:T(8,128)(2,1)S(1)}, bf16[2,32,128]{2,1,0:T(8,128)(2,1)S(1)}, u32[]{:S(2)}, u32[]{:S(2)}) collective-permute-start(bf16[2,32,128]{2,1,0:T(8,128)(2,1)S(1)} %get-tuple-element.120), channel_id=1, source_target_pairs={{0,16},{8,24},{16,0},{24,8},{1,17},{9,25},{17,1},{25,9},{2,18},{10... | collective-permute-start | bytes 49160 | tf_op jit(solution)/shard_map/ppermute | solution.py:115
  42.0 3.3 %collective-permute-start.10 = (bf16[2,32,128]{2,1,0:T(8,128)(2,1)S(1)}, bf16[2,32,128]{2,1,0:T(8,128)(2,1)S(1)}, u32[]{:S(2)}, u32[]{:S(2)}) collective-permute-start(bf16[2,32,128]{2,1,0:T(8,128)(2,1)S(1)} %get-tuple-element.121), channel_id=1, source_target_pairs={{0,24},{8,16},{16,8},{24,0},{1,25},{9,17},{17,9},{25,1},{2,26},{10... | collective-permute-start | bytes 49160 | tf_op jit(solution)/shard_map/ppermute | solution.py:115
  45.3 7.4 %collective-permute-start.13 = (bf16[4,2,32,128]{3,2,1,0:T(8,128)(2,1)S(1)}, bf16[4,2,32,128]{3,2,1,0:T(8,128)(2,1)S(1)}, u32[]{:S(2)}, u32[]{:S(2)}) collective-permute-start(bf16[4,2,32,128]{3,2,1,0:T(8,128)(2,1)S(1)} %shard_map.185.refs_0_), channel_id=1, source_target_pairs={{0,3},{1,2},{2,1},{3,0},{4,7},{5,6},{6,5},{7,4},{8,11},{9,10},{10,... | collective-permute-start | bytes 196616 | tf_op jit(solution)/shard_map/ppermute | solution.py:115
  46.1 7.6 %collective-permute-start.12 = (bf16[4,2,32,128]{3,2,1,0:T(8,128)(2,1)S(1)}, bf16[4,2,32,128]{3,2,1,0:T(8,128)(2,1)S(1)}, u32[]{:S(2)}, u32[]{:S(2)}) collective-permute-start(bf16[4,2,32,128]{3,2,1,0:T(8,128)(2,1)S(1)} %shard_map.185.refs_0_), channel_id=1, source_target_pairs={{0,2},{1,3},{2,0},{3,1},{4,6},{5,7},{6,4},{7,5},{8,10},{9,11},{10,... | collective-permute-start | bytes 196616 | tf_op jit(solution)/shard_map/ppermute | solution.py:115
  47.2 6.5 %collective-permute-start.11 = (bf16[4,2,32,128]{3,2,1,0:T(8,128)(2,1)S(1)}, bf16[4,2,32,128]{3,2,1,0:T(8,128)(2,1)S(1)}, u32[]{:S(2)}, u32[]{:S(2)}) collective-permute-start(bf16[4,2,32,128]{3,2,1,0:T(8,128)(2,1)S(1)} %shard_map.185.refs_0_), channel_id=1, source_target_pairs={{0,1},{1,0},{2,3},{3,2},{4,5},{5,4},{6,7},{7,6},{8,9},{9,8},{10,11... | collective-permute-start | bytes 196616 | tf_op jit(solution)/shard_map/ppermute | solution.py:115

commit v3 on v2

--- a/solution.py
+++ b/solution.py
@@ -358,30 +358,29 @@
 
         def other_values_seen(weighted, first_weight_ref, weight, lifted, cross_stats_ref, *refs):
             values, stores = refs[:others], refs[others : 2 * others]
-            attended_ref, stats, packed = refs[2 * others :]
+            attended_ref, packed = refs[2 * others :]
             attended = weighted[...] * first_weight_ref[...]
             for by in range(others):
                 attended = attended + dot_tn(values[by][...], stores[by][...]) * weight[by : by + 1, :]
             attended_ref[...] = attended
             squares, slopes = statistics(attended, lifted[...])
-            stats[0:1, :], stats[1:2, :] = squares, slopes
             lines = [squares, slopes, cross_stats_ref[0:1, :], cross_stats_ref[1:2, :]]
             halves = [entry[:, at : at + half] for entry in lines for at in (0, half)]
             tile = jnp.concatenate(halves, axis=0)
             for at in range(peers):
                 packed[at] = tile.astype(BF16)
 
-        self_attended, self_stats, packed = call(
+        self_attended, packed = call(
             other_values_seen,
             [first_weighted, first_weight, other_weight, self_lifted, cross_stats] + other_values + other_stores,
-            [(tall, F32), ((2, frames), F32), ((peers, 8, half), BF16)],
+            [(tall, F32), ((peers, 8, half), BF16)],
             flops=frames * unit * others,
         )
 
 
         received = [lax.all_to_all(packed, ("sec", "tp"), split_axis=0, concat_axis=0, tiled=True)]
 
-        def norm_terms(received_ref, stats, attended, lifted, at):
+        def norm_terms(received_ref, attended, lifted, at):
             sums = received_ref[0][0].astype(F32)
             for source in range(1, peers):
                 sums = sums + received_ref[0][source].astype(F32)
@@ -393,7 +392,8 @@
             slope = joined[1] / full_width
             curve = scale * scale * slope
             grad = scale * (lifted[...] - attended[...] * curve)
-            delta = scale * (stats[1:2, :] - curve * stats[0:1, :])
+            rounded = grad.astype(BF16).astype(F32)
+            delta = jnp.sum(rounded * attended[...], axis=0, keepdims=True)
             return scale, delta, grad
 
         def block_grads(key_grad, value_grad, value, store, weight, delta, grad_tall, grad_folded, query, slopes):
@@ -430,12 +430,12 @@
             )
 
         def cross_backward(*refs):
-            received_ref, (stats, attended, lifted, weight, query) = refs[:1], refs[1:6]
-            refs = refs[6:]
+            received_ref, (attended, lifted, weight, query) = refs[:1], refs[1:5]
+            refs = refs[5:]
             blocks, stores = refs[:others], refs[others : 2 * others]
             sums, slopes = refs[2 * others : 3 * others], refs[3 * others : 4 * others]
             scale_ref, delta_ref, grad_ref = refs[4 * others :]
-            scale, delta, grad = norm_terms(received_ref, stats, attended, lifted, 1)
+            scale, delta, grad = norm_terms(received_ref, attended, lifted, 1)
             scale_ref[...], delta_ref[...], grad_ref[...] = scale, delta, grad
             for by in range(others):
                 factor = weight[by + 1 : by + 2, :]
@@ -444,7 +444,7 @@
         results = call(
             cross_backward,
             received
-            + [cross_stats, cross_attended, cross_lifted, cross_weight, cross_query]
+            + [cross_attended, cross_lifted, cross_weight, cross_query]
             + memories[1:]
             + cross_stores[1:],
             [((2, group, columns), BF16)] * others
@@ -505,12 +505,12 @@
         )
 
         def other_backward(*refs):
-            received_ref, (stats, attended, lifted, weight, query) = refs[:1], refs[1:6]
-            refs = refs[6:]
+            received_ref, (attended, lifted, weight, query) = refs[:1], refs[1:5]
+            refs = refs[5:]
             values, stores = refs[:others], refs[others : 2 * others]
             pairs_out, slopes = refs[2 * others : 3 * others], refs[3 * others : 4 * others]
             grad_ref, scale_ref, delta_ref = refs[4 * others :]
-            scale, delta, grad = norm_terms(received_ref, stats, attended, lifted, 0)
+            scale, delta, grad = norm_terms(received_ref, attended, lifted, 0)
             scale_ref[...], delta_ref[...], grad_ref[...] = scale, delta, grad
             grad_tall = grad.astype(BF16)
             for by in range(others):
@@ -539,7 +539,7 @@
         results = call(
             other_backward,
             received
-            + [self_stats, self_attended, self_lifted, other_weight, self_query]
+            + [self_attended, self_lifted, other_weight, self_query]
             + other_values
             + list(other_stores),
             [((2,) + wide, BF16)] * others

time: 55.4 us -> 55.4 us (level)
  no operation moved by 1% of the time
where the time goes in v3:
time: 55.4 us; the launch traced here: 55.2 us
  waiting for transfers between devices  16.6 us (30%)
  starting transfers between devices  15.5 us (28%)
  blocking collectives  11.7 us (21%)
  Pallas kernels  10.5 us (19%)
  between operations  0.76 us (1%)
    ppermute x5, waiting for transfers between devices, shifted(): lax.ppermute(value, axis, [(at, (at + by) % count) for at in range(count)])  12.3 us
    all_to_all x1, blocking collectives, per_device(): lax.all_to_all(packed, ('sec', 'tp'), split_axis=0, concat_axis=0, tiled=...  11.7 us
    pallas_call x17, Pallas kernels, call(): pl.pallas_call(body, out_shape=shapes, in_specs=[SMEM] * smem + [space] *...  10.5 us
    ppermute x9, starting transfers between devices, swapped(): return lax.ppermute(value, axis, [(at, at ^ by) for at in range(count)])  8.31 us
    ppermute x5, starting transfers between devices, shifted(): lax.ppermute(value, axis, [(at, (at + by) % count) for at in range(count)])  7.21 us
    ppermute x9, waiting for transfers between devices, swapped(): return lax.ppermute(value, axis, [(at, at ^ by) for at in range(count)])  4.35 us
  transfers between devices with their start and end apart: 14, of which 5 were waited for; matrix products, arithmetic and copies ran while one was open for 0% of the time, Pallas kernels for 15%

profile of v3, /device:TPU:0, one launch (start us, length us, event | category | flops | bytes accessed | tf_op | source)
XLA Modules:
  0.0 55.2 jit_solution(10112092076120916096)
XLA Ops:
  0.6 3.0 %collective-permute-start = (bf16[512,128]{1,0:T(8,128)(2,1)}, bf16[512,128]{1,0:T(8,128)(2,1)S(1)}, u32[]{:S(2)}, u32[]{:S(2)}) collective-permute-start(bf16[512,128]{1,0:T(8,128)(2,1)} %refs_1_.1), channel_id=1, source_target_pairs={{0,4},{4,0},{1,5},{5,1},{2,6},{6,2},{3,7},{7,3},{8,12},{12,8},{9,1... | collective-permute-start | bytes 393224 | tf_op jit(solution)/shard_map/ppermute | solution.py:105
  3.7 0.9 %shard_map.173.refs_0_ = bf16[4,2,32,128]{3,2,1,0:T(8,128)(2,1)S(1)} custom-call(bf16[32,2048]{1,0:T(8,128)(2,1)} %key_ref.1, bf16[32,2048]{1,0:T(8,128)(2,1)} %value_ref.1), custom_call_target="tpu_custom_call" | custom-call | bytes 327680 | tf_op jit(solution)/shard_map/pallas_call | solution.py:43
  4.6 2.0 %collective-permute-start.1 = (bf16[4,2,32,128]{3,2,1,0:T(8,128)(2,1)S(1)}, bf16[4,2,32,128]{3,2,1,0:T(8,128)(2,1)S(1)}, u32[]{:S(2)}, u32[]{:S(2)}) collective-permute-start(bf16[4,2,32,128]{3,2,1,0:T(8,128)(2,1)S(1)} %shard_map.173.refs_0_), channel_id=1, source_target_pairs={{0,4},{4,0},{1,5},{5,1},{2,6},{6,2},{3,7},{7,3},{8,12},{12,8},{9,1... | collective-permute-start | bytes 196616 | tf_op jit(solution)/shard_map/ppermute | solution.py:105
  6.6 4.9 %collective-permute-done.1.refs_1_ = bf16[4,2,32,128]{3,2,1,0:T(8,128)(2,1)S(1)} collective-permute-done((bf16[4,2,32,128]{3,2,1,0:T(8,128)(2,1)S(1)}, bf16[4,2,32,128]{3,2,1,0:T(8,128)(2,1)S(1)}, u32[]{:S(2)}, u32[]{:S(2)}) %collective-permute-start.1) | collective-permute-done | bytes 65568 | tf_op jit(solution)/shard_map/ppermute | solution.py:105
  11.7 1.8 %collective-permute-start.3 = (bf16[2,2,32,128]{3,2,1,0:T(8,128)(2,1)S(1)}, bf16[2,2,32,128]{3,2,1,0:T(8,128)(2,1)S(1)}, u32[]{:S(2)}, u32[]{:S(2)}) collective-permute-start(bf16[2,2,32,128]{3,2,1,0:T(8,128)(2,1)S(1)} %get-tuple-element.83), channel_id=1, source_target_pairs={{0,16},{8,24},{16,0},{24,8},{1,17},{9,25},{17,1},{25,9},{2,18},{10... | collective-permute-start | bytes 98312 | tf_op jit(solution)/shard_map/ppermute | solution.py:115
  13.6 1.3 %shard_map.170 = (bf16[512,128]{1,0:T(8,128)(2,1)S(1)}, bf16[512,128]{1,0:T(8,128)(2,1)S(1)}, bf16[512,128]{1,0:T(8,128)(2,1)S(1)}, bf16[512,128]{1,0:T(8,128)(2...) custom-call(s32[8]{0:T(128)} %start_ref.1, ...), custom_call_target="tpu_custom_call" | custom-call | bytes 1591328 | tf_op jit(solution)/shard_map/pallas_call | solution.py:43
  14.8 0.8 %shard_map.171 = (bf16[512,512]{1,0:T(8,128)(2,1)S(1)}, f32[1,512]{1,0:T(1,128)S(1)}, f32[1,512]{1,0:T(1,128)S(1)}, f32[128,512]{1,0:T(8,128)S(1)}, f32[128,512]{1,0:T(8,128)S(1)}, /*index=5*/f32[128,512]{1,0:T(8,128)S(1)}) custom-call(s32[8,512]{1,0:T(8,128)S(1)} %get-tuple-element.65.base, bf16[512,128]{1,0:T(8,128)(2,1)S(1)} %get-tuple-element.66.query.refs_4_, ...), custom_call_target="tpu_custom_call" | custom-call | flops 134217728 | bytes 1987584 | tf_op jit(solution)/shard_map/pallas_call | solution.py:43
  15.7 1.2 %collective-permute-done.4.refs_3_ = bf16[2,2,32,128]{3,2,1,0:T(8,128)(2,1)S(1)} collective-permute-done((bf16[2,2,32,128]{3,2,1,0:T(8,128)(2,1)S(1)}, bf16[2,2,32,128]{3,2,1,0:T(8,128)(2,1)S(1)}, u32[]{:S(2)}, u32[]{:S(2)}) %collective-permute-start.4) | collective-permute-done | bytes 32800 | tf_op jit(solution)/shard_map/ppermute | solution.py:115
  16.9 0.6 %shard_map.176 = (bf16[128,512]{1,0:T(8,128)(2,1)S(1)}, bf16[128,512]{1,0:T(8,128)(2,1)S(1)}, f32[2,512]{1,0:T(2,128)S(1)}, f32[128,512]{1,0:T(8,128)S(1)}, f32[2,512]{1,0:T(2,128)S(1)}) custom-call(bf16[512,128]{1,0:T(8,128)(2,1)S(1)} %get-tuple-element.79.query.refs_4_, f32[128,512]{1,0:T(8,128)S(1)} %get-tuple-element.80.lifted.refs_2_, ...), custom_call_target="tpu_custom_call" | custom-call | flops 67108864 | bytes 1056768 | tf_op jit(solution)/shard_map/pallas_call | solution.py:43
  18.3 11.7 %all_to_all.5.refs_0_ = bf16[16,8,256]{2,1,0:T(8,128)(2,1)S(1)} all-to-all(bf16[16,8,256]{2,1,0:T(8,128)(2,1)S(1)} %get-tuple-element.89), channel_id=1, replica_groups=mesh['sec'=4,'ctx'=2,'tp'=4] {'sec','tp'}, dimensions={0} | all-to-all | bytes 131072 | tf_op jit(solution)/shard_map/all_to_all | solution.py:381
  30.4 1.0 %shard_map.179 = (bf16[2,512,128]{2,1,0:T(8,128)(2,1)S(1)}, bf16[512,512]{1,0:T(8,128)(2,1)S(1)}, f32[128,512]{1,0:T(8,128)S(1)}, f32[1,512]{1,0:T(1,128)S(1)}, f32[1,512]{1,0:T(1,128)S(1)}) custom-call(bf16[16,8,256]{2,1,0:T(8,128)(2,1)S(1)} %all_to_all.5.refs_0_, f32[128,512]{1,0:T(8,128)S(1)} %get-tuple-element.90.refs_1_.attended, ...), custom_call_target="tpu_custom_call" | custom-call | flops 201326592 | bytes 2430976 | tf_op jit(solution)/shard_map/pallas_call | solution.py:43
  31.4 1.6 %collective-permute-start.6 = (bf16[2,512,128]{2,1,0:T(8,128)(2,1)S(1)}, bf16[2,512,128]{2,1,0:T(8,128)(2,1)S(1)}, u32[]{:S(2)}, u32[]{:S(2)}) collective-permute-start(bf16[2,512,128]{2,1,0:T(8,128)(2,1)S(1)} %get-tuple-element.110), channel_id=1, source_target_pairs={{0,4},{4,0},{1,5},{5,1},{2,6},{6,2},{3,7},{7,3},{8,12},{12,8},{9,1... | collective-permute-start | bytes 786440 | tf_op jit(solution)/shard_map/ppermute | solution.py:105
  33.9 7.3 %collective-permute-done.7.refs_1_ = bf16[2,128,128]{2,1,0:T(8,128)(2,1)S(1)} collective-permute-done((bf16[2,128,128]{2,1,0:T(8,128)(2,1)S(1)}, bf16[2,128,128]{2,1,0:T(8,128)(2,1)S(1)}, u32[]{:S(2)}, u32[]{:S(2)}) %collective-permute-start.7) | collective-permute-done | bytes 65568 | tf_op jit(solution)/shard_map/ppermute | solution.py:105
  41.3 0.6 %collective-permute-start.9 = (bf16[2,32,128]{2,1,0:T(8,128)(2,1)S(1)}, bf16[2,32,128]{2,1,0:T(8,128)(2,1)S(1)}, u32[]{:S(2)}, u32[]{:S(2)}) collective-permute-start(bf16[2,32,128]{2,1,0:T(8,128)(2,1)S(1)} %get-tuple-element.118), channel_id=1, source_target_pairs={{0,16},{8,24},{16,0},{24,8},{1,17},{9,25},{17,1},{25,9},{2,18},{10... | collective-permute-start | bytes 49160 | tf_op jit(solution)/shard_map/ppermute | solution.py:115
  42.0 1.2 %collective-permute-start.10 = (bf16[2,32,128]{2,1,0:T(8,128)(2,1)S(1)}, bf16[2,32,128]{2,1,0:T(8,128)(2,1)S(1)}, u32[]{:S(2)}, u32[]{:S(2)}) collective-permute-start(bf16[2,32,128]{2,1,0:T(8,128)(2,1)S(1)} %get-tuple-element.119), channel_id=1, source_target_pairs={{0,24},{8,16},{16,8},{24,0},{1,25},{9,17},{17,9},{25,1},{2,26},{10... | collective-permute-start | bytes 49160 | tf_op jit(solution)/shard_map/ppermute | solution.py:115
  43.2 2.1 %collective-permute-done.9.refs_2_ = bf16[2,32,128]{2,1,0:T(8,128)(2,1)S(1)} collective-permute-done((bf16[2,32,128]{2,1,0:T(8,128)(2,1)S(1)}, bf16[2,32,128]{2,1,0:T(8,128)(2,1)S(1)}, u32[]{:S(2)}, u32[]{:S(2)}) %collective-permute-start.9) | collective-permute-done | bytes 16416 | tf_op jit(solution)/shard_map/ppermute | solution.py:115
  45.3 0.8 %collective-permute-start.13 = (bf16[4,2,32,128]{3,2,1,0:T(8,128)(2,1)S(1)}, bf16[4,2,32,128]{3,2,1,0:T(8,128)(2,1)S(1)}, u32[]{:S(2)}, u32[]{:S(2)}) collective-permute-start(bf16[4,2,32,128]{3,2,1,0:T(8,128)(2,1)S(1)} %shard_map.185.refs_0_), channel_id=1, source_target_pairs={{0,3},{1,2},{2,1},{3,0},{4,7},{5,6},{6,5},{7,4},{8,11},{9,10},{10,... | collective-permute-start | bytes 196616 | tf_op jit(solution)/shard_map/ppermute | solution.py:115
  46.1 1.1 %collective-permute-start.12 = (bf16[4,2,32,128]{3,2,1,0:T(8,128)(2,1)S(1)}, bf16[4,2,32,128]{3,2,1,0:T(8,128)(2,1)S(1)}, u32[]{:S(2)}, u32[]{:S(2)}) collective-permute-start(bf16[4,2,32,128]{3,2,1,0:T(8,128)(2,1)S(1)} %shard_map.185.refs_0_), channel_id=1, source_target_pairs={{0,2},{1,3},{2,0},{3,1},{4,6},{5,7},{6,4},{7,5},{8,10},{9,11},{10,... | collective-permute-start | bytes 196616 | tf_op jit(solution)/shard_map/ppermute | solution.py:115
  47.2 2.6 %collective-permute-start.11 = (bf16[4,2,32,128]{3,2,1,0:T(8,128)(2,1)S(1)}, bf16[4,2,32,128]{3,2,1,0:T(8,128)(2,1)S(1)}, u32[]{:S(2)}, u32[]{:S(2)}) collective-permute-start(bf16[4,2,32,128]{3,2,1,0:T(8,128)(2,1)S(1)} %shard_map.185.refs_0_), channel_id=1, source_target_pairs={{0,1},{1,0},{2,3},{3,2},{4,5},{5,4},{6,7},{7,6},{8,9},{9,8},{10,11... | collective-permute-start | bytes 196616 | tf_op jit(solution)/shard_map/ppermute | solution.py:115
  49.8 1.0 %shard_map.182 = (bf16[512,128]{1,0:T(8,128)(2,1)}, bf16[512,128]{1,0:T(8,128)(2,1)}) custom-call(f32[1,512]{1,0:T(1,128)S(1)} %get-tuple-element.94.refs_7_.scale, f32[1,128]{1,0:T(1,128)S(1)} %get-tuple-element.71.cross_gain_ref.gain, f32[128,512]{1,0:T(8,128)S(1)} %get-tuple-element.91.refs_1_.attended, ...), custom_call_target="tpu_custom_call" | custom-call | flops 33554432 | bytes 920064 | tf_op jit(solution)/shard_map/pallas_call | solution.py:43
  50.8 1.9 %shard_map.180 = (f32[512,128]{1,0:T(8,128)S(1)}, f32[512,128]{1,0:T(8,128)S(1)}, bf16[512,128]{1,0:T(8,128)(2,1)}, bf16[512,128]{1,0:T(8,128)(2,1)}) custom-call(f32[128,512]{1,0:T(8,128)S(1)} %get-tuple-element.95.grad, f32[1,512]{1,0:T(1,128)S(1)} %get-tuple-element.96.scale, f32[1,512]{1,0:T(1,128)S(1)} %get-tuple-element.97.delta, ...), custom_call_target="tpu_custom_call" | custom-call | flops 335544320 | bytes 2890240 | tf_op jit(solution)/shard_map/pallas_call | solution.py:43
  52.7 1.0 %collective-permute-done.12.refs_2_ = bf16[4,2,32,128]{3,2,1,0:T(8,128)(2,1)S(1)} collective-permute-done((bf16[4,2,32,128]{3,2,1,0:T(8,128)(2,1)S(1)}, bf16[4,2,32,128]{3,2,1,0:T(8,128)(2,1)S(1)}, u32[]{:S(2)}, u32[]{:S(2)}) %collective-permute-start.12) | collective-permute-done | bytes 65568 | tf_op jit(solution)/shard_map/ppermute | solution.py:115
  53.7 0.8 %shard_map.186 = (bf16[32,2048]{1,0:T(8,128)(2,1)}, bf16[32,2048]{1,0:T(8,128)(2,1)}) custom-call(bf16[4,2,32,128]{3,2,1,0:T(8,128)(2,1)S(1)} %shard_map.185.refs_0_, bf16[4,2,32,128]{3,2,1,0:T(8,128)(2,1)S(1)} %collective-permute-done.11.refs_1_, bf16[4,2,32,128]{3,2,1,0:T(8,128)(2,1)S(1)} %collective-permute-done.12.refs_2_, ...), custom_call_target="tpu_custom_call" | custom-call | bytes 524288 | tf_op jit(solution)/shard_map/pallas_call | solution.py:43
  54.4 0.7 %shard_map.183 = (bf16[512,128]{1,0:T(8,128)(2,1)}, bf16[512,128]{1,0:T(8,128)(2,1)}) custom-call(f32[512,128]{1,0:T(8,128)S(1)} %get-tuple-element.108.own_key_ref, f32[512,128]{1,0:T(8,128)S(1)} %get-tuple-element.109.own_value_ref, bf16[2,512,128]{2,1,0:T(8,128)(2,1)S(1)} %collective-permute-done.6.refs_0_), custom_call_target="tpu_custom_call" | custom-call | bytes 1048576 | tf_op jit(solution)/shard_map/pallas_call | solution.py:43
  (22 shorter events, 2.5 us)
Async XLA Ops:
  0.6 16.8 %collective-permute-start = (bf16[512,128]{1,0:T(8,128)(2,1)}, bf16[512,128]{1,0:T(8,128)(2,1)S(1)}, u32[]{:S(2)}, u32[]{:S(2)}) collective-permute-start(bf16[512,128]{1,0:T(8,128)(2,1)} %refs_1_.1), channel_id=1, source_target_pairs={{0,4},{4,0},{1,5},{5,1},{2,6},{6,2},{3,7},{7,3},{8,12},{12,8},{9,1... | collective-permute-start | bytes 393224 | tf_op jit(solution)/shard_map/ppermute | solution.py:105
  3.7 14.3 %collective-permute-start.5 = (bf16[512,128]{1,0:T(8,128)(2,1)}, bf16[512,128]{1,0:T(8,128)(2,1)S(1)}, u32[]{:S(2)}, u32[]{:S(2)}) collective-permute-start(bf16[512,128]{1,0:T(8,128)(2,1)} %refs_2_.1), channel_id=1, source_target_pairs={{0,4},{4,0},{1,5},{5,1},{2,6},{6,2},{3,7},{7,3},{8,12},{12,8},{9,1... | collective-permute-start | bytes 393224 | tf_op jit(solution)/shard_map/ppermute | solution.py:105
  4.6 7.0 %collective-permute-start.1 = (bf16[4,2,32,128]{3,2,1,0:T(8,128)(2,1)S(1)}, bf16[4,2,32,128]{3,2,1,0:T(8,128)(2,1)S(1)}, u32[]{:S(2)}, u32[]{:S(2)}) collective-permute-start(bf16[4,2,32,128]{3,2,1,0:T(8,128)(2,1)S(1)} %shard_map.173.refs_0_), channel_id=1, source_target_pairs={{0,4},{4,0},{1,5},{5,1},{2,6},{6,2},{3,7},{7,3},{8,12},{12,8},{9,1... | collective-permute-start | bytes 196616 | tf_op jit(solution)/shard_map/ppermute | solution.py:105
  11.6 4.0 %collective-permute-start.2 = (bf16[2,2,32,128]{3,2,1,0:T(8,128)(2,1)S(1)}, bf16[2,2,32,128]{3,2,1,0:T(8,128)(2,1)S(1)}, u32[]{:S(2)}, u32[]{:S(2)}) collective-permute-start(bf16[2,2,32,128]{3,2,1,0:T(8,128)(2,1)S(1)} %get-tuple-element.82), channel_id=1, source_target_pairs={{0,8},{8,0},{16,24},{24,16},{1,9},{9,1},{17,25},{25,17},{2,10},{10... | collective-permute-start | bytes 98312 | tf_op jit(solution)/shard_map/ppermute | solution.py:115
  11.7 4.0 %collective-permute-start.3 = (bf16[2,2,32,128]{3,2,1,0:T(8,128)(2,1)S(1)}, bf16[2,2,32,128]{3,2,1,0:T(8,128)(2,1)S(1)}, u32[]{:S(2)}, u32[]{:S(2)}) collective-permute-start(bf16[2,2,32,128]{3,2,1,0:T(8,128)(2,1)S(1)} %get-tuple-element.83), channel_id=1, source_target_pairs={{0,16},{8,24},{16,0},{24,8},{1,17},{9,25},{17,1},{25,9},{2,18},{10... | collective-permute-start | bytes 98312 | tf_op jit(solution)/shard_map/ppermute | solution.py:115
  13.5 3.4 %collective-permute-start.4 = (bf16[2,2,32,128]{3,2,1,0:T(8,128)(2,1)S(1)}, bf16[2,2,32,128]{3,2,1,0:T(8,128)(2,1)S(1)}, u32[]{:S(2)}, u32[]{:S(2)}) collective-permute-start(bf16[2,2,32,128]{3,2,1,0:T(8,128)(2,1)S(1)} %get-tuple-element.84), channel_id=1, source_target_pairs={{0,24},{8,16},{16,8},{24,0},{1,25},{9,17},{17,9},{25,1},{2,26},{10... | collective-permute-start | bytes 98312 | tf_op jit(solution)/shard_map/ppermute | solution.py:115
  31.4 23.0 %collective-permute-start.6 = (bf16[2,512,128]{2,1,0:T(8,128)(2,1)S(1)}, bf16[2,512,128]{2,1,0:T(8,128)(2,1)S(1)}, u32[]{:S(2)}, u32[]{:S(2)}) collective-permute-start(bf16[2,512,128]{2,1,0:T(8,128)(2,1)S(1)} %get-tuple-element.110), channel_id=1, source_target_pairs={{0,4},{4,0},{1,5},{5,1},{2,6},{6,2},{3,7},{7,3},{8,12},{12,8},{9,1... | collective-permute-start | bytes 786440 | tf_op jit(solution)/shard_map/ppermute | solution.py:105
  33.0 8.2 %collective-permute-start.7 = (bf16[2,128,128]{2,1,0:T(8,128)(2,1)S(1)}, bf16[2,128,128]{2,1,0:T(8,128)(2,1)S(1)}, u32[]{:S(2)}, u32[]{:S(2)}) collective-permute-start(bf16[2,128,128]{2,1,0:T(8,128)(2,1)S(1)} %get-tuple-element.115), channel_id=1, source_target_pairs={{0,4},{4,0},{1,5},{5,1},{2,6},{6,2},{3,7},{7,3},{8,12},{12,8},{9,1... | collective-permute-start | bytes 196616 | tf_op jit(solution)/shard_map/ppermute | solution.py:105
  41.3 1.9 %collective-permute-start.8 = (bf16[2,32,128]{2,1,0:T(8,128)(2,1)S(1)}, bf16[2,32,128]{2,1,0:T(8,128)(2,1)S(1)}, u32[]{:S(2)}, u32[]{:S(2)}) collective-permute-start(bf16[2,32,128]{2,1,0:T(8,128)(2,1)S(1)} %get-tuple-element.117), channel_id=1, source_target_pairs={{0,8},{8,0},{16,24},{24,16},{1,9},{9,1},{17,25},{25,17},{2,10},{10... | collective-permute-start | bytes 49160 | tf_op jit(solution)/shard_map/ppermute | solution.py:115
  41.3 4.0 %collective-permute-start.9 = (bf16[2,32,128]{2,1,0:T(8,128)(2,1)S(1)}, bf16[2,32,128]{2,1,0:T(8,128)(2,1)S(1)}, u32[]{:S(2)}, u32[]{:S(2)}) collective-permute-start(bf16[2,32,128]{2,1,0:T(8,128)(2,1)S(1)} %get-tuple-element.118), channel_id=1, source_target_pairs={{0,16},{8,24},{16,0},{24,8},{1,17},{9,25},{17,1},{25,9},{2,18},{10... | collective-permute-start | bytes 49160 | tf_op jit(solution)/shard_map/ppermute | solution.py:115
  42.0 3.3 %collective-permute-start.10 = (bf16[2,32,128]{2,1,0:T(8,128)(2,1)S(1)}, bf16[2,32,128]{2,1,0:T(8,128)(2,1)S(1)}, u32[]{:S(2)}, u32[]{:S(2)}) collective-permute-start(bf16[2,32,128]{2,1,0:T(8,128)(2,1)S(1)} %get-tuple-element.119), channel_id=1, source_target_pairs={{0,24},{8,16},{16,8},{24,0},{1,25},{9,17},{17,9},{25,1},{2,26},{10... | collective-permute-start | bytes 49160 | tf_op jit(solution)/shard_map/ppermute | solution.py:115
  45.3 7.4 %collective-permute-start.13 = (bf16[4,2,32,128]{3,2,1,0:T(8,128)(2,1)S(1)}, bf16[4,2,32,128]{3,2,1,0:T(8,128)(2,1)S(1)}, u32[]{:S(2)}, u32[]{:S(2)}) collective-permute-start(bf16[4,2,32,128]{3,2,1,0:T(8,128)(2,1)S(1)} %shard_map.185.refs_0_), channel_id=1, source_target_pairs={{0,3},{1,2},{2,1},{3,0},{4,7},{5,6},{6,5},{7,4},{8,11},{9,10},{10,... | collective-permute-start | bytes 196616 | tf_op jit(solution)/shard_map/ppermute | solution.py:115
  46.1 7.6 %collective-permute-start.12 = (bf16[4,2,32,128]{3,2,1,0:T(8,128)(2,1)S(1)}, bf16[4,2,32,128]{3,2,1,0:T(8,128)(2,1)S(1)}, u32[]{:S(2)}, u32[]{:S(2)}) collective-permute-start(bf16[4,2,32,128]{3,2,1,0:T(8,128)(2,1)S(1)} %shard_map.185.refs_0_), channel_id=1, source_target_pairs={{0,2},{1,3},{2,0},{3,1},{4,6},{5,7},{6,4},{7,5},{8,10},{9,11},{10,... | collective-permute-start | bytes 196616 | tf_op jit(solution)/shard_map/ppermute | solution.py:115
  47.2 6.5 %collective-permute-start.11 = (bf16[4,2,32,128]{3,2,1,0:T(8,128)(2,1)S(1)}, bf16[4,2,32,128]{3,2,1,0:T(8,128)(2,1)S(1)}, u32[]{:S(2)}, u32[]{:S(2)}) collective-permute-start(bf16[4,2,32,128]{3,2,1,0:T(8,128)(2,1)S(1)} %shard_map.185.refs_0_), channel_id=1, source_target_pairs={{0,1},{1,0},{2,3},{3,2},{4,5},{5,4},{6,7},{7,6},{8,9},{9,8},{10,11... | collective-permute-start | bytes 196616 | tf_op jit(solution)/shard_map/ppermute | solution.py:115
